TPU v7x, 256 devices: a whole 4x4x8 slice. The times are simulated.
256 devices in a mesh: atoms: 16 (over x, y), cols: 16 (over z, core).
Axes of the slice: x: 4, y: 4, z: 8, core: 2. Of those that a mesh axis runs over, the one named last changes fastest.
Arguments:
- supports: bfloat16 [256, 4, 27, 16, 256], P('atoms', None, None, 'cols'), may hold values from -0.012 to 0.012
- potential: bfloat16 [256, 27, 16, 256], P('atoms', None, 'cols'), may hold values from 0.1 to 4.5
- anchors: int32 [256, 3], replicated, may hold values from 0 to 47, as said below
- kernel: float32 [1024, 1024], P('atoms', 'cols'), may hold values from -0.04 to 1.1
Outputs:
- metric: float32 [1024, 1024], P('atoms', 'cols')
- hamiltonian: float32 [1024, 1024], P('atoms', 'cols')
- purified: float32 [1024, 1024], P('atoms', 'cols')
Inputs may be any that keep to these rules, and one draw needn't show every extreme that they name: `anchors`: the first component of atom a's anchor lies in 3 (a // 16) to 3 (a // 16) + 2, the second and third in 0 to 3.
All inputs are finite; a program needn't handle non-finite values.
Results may differ from a plain program's by a relative error of at most 0.0003.
Values may be sent and summed in bfloat16 or wider, within the bound.
A program may use at most 128 MiB of HBM per device.

v0:
```python
import functools

import jax
import jax.numpy as jnp
from jax import lax
from jax.experimental import pallas as pl
from jax.experimental.pallas import tpu as pltpu
from jax.sharding import PartitionSpec as P

MESH = pl.DeviceIdType.MESH
F32 = jnp.float32
BF16 = jnp.bfloat16
GRID_BLOCKS = 180
ATOMS = 16
FUNCS = 4
ROWS = ATOMS * FUNCS


def split(a):
    high = a.astype(BF16)
    return high, (a - high.astype(F32)).astype(BF16)


def dot3(left, right, dims=(((1,), (0,)), ((), ()))):
    lh, ll = left
    rh, rl = right
    mm = functools.partial(lax.dot_general, dimension_numbers=dims, preferred_element_type=F32)
    return mm(lh, rh) + (mm(lh, rl) + mm(ll, rh))


def shift_matrices():
    source = lax.broadcasted_iota(jnp.int32, (256, 256), 0)
    target = lax.broadcasted_iota(jnp.int32, (256, 256), 1)
    step = target - source
    z = target % 16
    one = jnp.float32(1.0)
    own = jnp.where(step == 0, -6.0, 0.0)
    own = own + jnp.where((step == 1) & (z != 0), one, 0.0)
    own = own + jnp.where((step == -1) & (z != 15), one, 0.0)
    own = own + jnp.where((step == 16) | (step == -16), one, 0.0)
    z_low = jnp.where((step == -15) & (z == 0), one, 0.0)
    z_high = jnp.where((step == 15) & (z == 15), one, 0.0)
    y_low = jnp.where(step == -240, one, 0.0)
    y_high = jnp.where(step == 240, one, 0.0)
    return [m.astype(BF16) for m in (own, z_low, z_high, y_low, y_high)]


def mm(a, b):
    return jnp.dot(a, b, preferred_element_type=F32)


def gram_kernel(sc, x_ref, lo_ref, hi_ref, bl_ref, bu_ref, v_ref, out_ref, grid, lap):
    def clear(g, carry):
        grid[g] = jnp.zeros((3 * ROWS, 256), BF16)
        return carry

    lax.fori_loop(0, GRID_BLOCKS + 1, clear, 0)
    own, z_low, z_high, y_low, y_high = shift_matrices()
    for bx in range(3):
        base = 9 * bx
        rows = lambda first, count: x_ref[base + first : base + first + count].reshape(count * ROWS, 256)
        lap[base : base + 9] = mm(rows(0, 9), own).reshape(9, ROWS, 256)
        for by in range(3):
            f = 3 * by
            lap[base + f + 1 : base + f + 3] += mm(rows(f, 2), z_low).reshape(2, ROWS, 256)
            lap[base + f : base + f + 2] += mm(rows(f + 1, 2), z_high).reshape(2, ROWS, 256)
        lap[base + 3 : base + 9] += mm(rows(0, 6), y_low).reshape(6, ROWS, 256)
        lap[base : base + 6] += mm(rows(3, 6), y_high).reshape(6, ROWS, 256)

    pick = (
        lax.broadcasted_iota(jnp.int32, (ROWS, ATOMS), 0) // FUNCS
        == lax.broadcasted_iota(jnp.int32, (ROWS, ATOMS), 1)
    ).astype(F32).astype(BF16)
    first, last = sc[48], sc[49]

    def place(p, carry):
        offset = (p // 9) * 36 + (p // 3 % 3) * 6 + p % 3
        values = x_ref[p].astype(F32)
        p_lo = p - 9 * first
        p_hi = p + 9 * last
        keep_lo = jnp.where(p_lo >= 0, 1.0, 0.0).astype(F32)
        keep_hi = jnp.where(p_hi < 27, 1.0, 0.0).astype(F32)
        low = lo_ref[jnp.maximum(p_lo, 0)].astype(F32) * keep_lo
        high = hi_ref[jnp.minimum(p_hi, 26)].astype(F32) * keep_hi
        pot = mm(pick, v_ref[p])
        hphi = (-0.5 * (lap[p] + low + high) + pot * values).astype(BF16)
        for a in range(ATOMS):
            g = sc[a] + offset
            grid[g, ROWS + 4 * a : ROWS + 4 * a + 4, :] = x_ref[p, 4 * a : 4 * a + 4, :]
            grid[g, 4 * a : 4 * a + 4, :] = hphi[4 * a : 4 * a + 4, :]
        return carry

    lax.fori_loop(0, 27, place, 0)

    def place_band(q, carry):
        offset = (q // 9) * 36 + (q // 3 % 3) * 6 + q % 3
        for a in range(ATOMS):
            g = sc[16 + a] + offset + 36
            g = jnp.where(g < 0, GRID_BLOCKS, g)
            grid[g, 2 * ROWS + 4 * a : 2 * ROWS + 4 * a + 4, :] = bl_ref[q, 4 * a : 4 * a + 4, :]
            g = sc[32 + a] + offset
            g = jnp.where(g >= GRID_BLOCKS, GRID_BLOCKS, g)
            grid[g, 2 * ROWS + 4 * a : 2 * ROWS + 4 * a + 4, :] = bu_ref[q, 4 * a : 4 * a + 4, :]
        return carry

    lax.fori_loop(0, 18, place_band, 0)

    def grams(start, count, columns):
        batch = 6

        def step(i, acc):
            g = start + batch * i
            left = jnp.concatenate([grid[g + k, 0 : 2 * ROWS] for k in range(batch)], axis=1)
            right = jnp.concatenate([grid[g + k, ROWS : ROWS + columns] for k in range(batch)], axis=1)
            return acc + lax.dot_general(left, right, (((1,), (1,)), ((), ())), preferred_element_type=F32)

        return lax.fori_loop(0, count // batch, step, jnp.zeros((2 * ROWS, columns), F32))

    lower = grams(0, 72, 2 * ROWS)
    middle = grams(72, 36, ROWS)
    upper = grams(108, 72, 2 * ROWS)
    total = jnp.concatenate(
        [lower[:, ROWS:], lower[:, :ROWS] + middle + upper[:, :ROWS], upper[:, ROWS:]], axis=1
    )
    for a in range(ATOMS):
        out_ref[a, 0:4, :] = total[ROWS + 4 * a : ROWS + 4 * a + 4, :]
        out_ref[a, 4:8, :] = total[4 * a : 4 * a + 4, :]


def gram(scalars, x, lo, hi, bl, bu, v):
    vmem = pl.BlockSpec(memory_space=pltpu.VMEM)
    return pl.pallas_call(
        gram_kernel,
        out_shape=jax.ShapeDtypeStruct((ATOMS, 8, 3 * ROWS), F32),
        in_specs=[pl.BlockSpec(memory_space=pltpu.SMEM)] + [vmem] * 6,
        out_specs=vmem,
        scratch_shapes=[
            pltpu.VMEM((GRID_BLOCKS + 1, 3 * ROWS, 256), BF16),
            pltpu.VMEM((27, ROWS, 256), F32),
        ],
        compiler_params=pltpu.CompilerParams(vmem_limit_bytes=60 * 1024 * 1024),
    )(scalars, x, lo, hi, bl, bu, v)


def purify_kernel(
    n, part, k0, mask, metric, ham, pur,
    rs_buf, piece, ag, k0row, k0n, bblk, ball, y1, y1all, k1, k1all, mrow, mall,
    rs_s, rs_r, ag_s, ag_r, kr_s, kr_r, kn_s, kn_r, b_s, b_r, y_s, y_r, k_s, k_r, m_s, m_r,
):
    s = lax.axis_index("atoms")
    c = lax.axis_index("cols")
    up = lambda base, k: lax.rem(base + k + 2 * n, n)
    e = up(c - s, 1)
    active = e < 3

    def remote(src, dst, ss, rs, row, col):
        return pltpu.make_async_remote_copy(
            src_ref=src, dst_ref=dst, send_sem=ss, recv_sem=rs, device_id=(row, col), device_id_type=MESH
        )

    barrier = pltpu.get_barrier_semaphore()

    def hello(row, col):
        pl.semaphore_signal(barrier, inc=1, device_id=(row, col), device_id_type=MESH)

    for k in range(1, n):
        hello(s, up(c, k))
        hello(up(s, k), c)
    pairs = [(d, f) for d in range(-2, 3) for f in range(3)]

    @pl.when(active)
    def _():
        for d, f in pairs:
            t, v = up(s, d), up(s, d + f - 1)
            if d != 0:

                @pl.when(v != c)
                def _():
                    hello(t, v)

    pl.semaphore_wait(barrier, 2 * (n - 1) + jnp.where(active, 10, 0))

    rs_copies = []
    for k in range(1, n):
        col = up(c, k)
        copy = remote(part.at[col], rs_buf.at[k - 1], rs_s.at[k - 1], rs_r.at[k - 1], s, col)
        copy.start()
        rs_copies.append(copy)
    kn_copies = []
    for i, d in enumerate((1, -1)):
        copy = remote(k0, k0n.at[i], kn_s.at[i], kn_r.at[i], up(s, d), c)
        copy.start()
        kn_copies.append(copy)
    kr_copies = []
    for k in range(1, n):
        copy = remote(k0, k0row.at[c], kr_s.at[k - 1], kr_r.at[k - 1], s, up(c, k))
        copy.start()
        kr_copies.append(copy)
    k0row[c] = k0[...]

    total = part[c]
    for k in range(1, n):
        rs_copies[k - 1].wait_recv()
        total = total + rs_buf[k - 1]
    piece[...] = total
    ag[c] = total
    ag_copies = []
    for k in range(1, n):
        copy = remote(piece, ag.at[c], ag_s.at[k - 1], ag_r.at[k - 1], s, up(c, k))
        copy.start()
        ag_copies.append(copy)
    for copy in kn_copies:
        copy.wait_recv()
    panel = split(jnp.concatenate([k0n[0], k0[...], k0n[1]], axis=0))
    for copy in ag_copies:
        copy.wait_recv()
    for a in range(ATOMS):
        mrow[4 * a : 4 * a + 4, :] = ag[a, 0:4, :]
    m_own = mrow[...]
    bblk[...] = dot3(split(m_own), panel)
    b_copies = []
    for k in range(1, n):
        copy = remote(bblk, ball.at[s], b_s.at[k - 1], b_r.at[k - 1], up(s, k), c)
        copy.start()
        b_copies.append(copy)
    ball[s] = bblk[...]
    m_sends = []
    for i, d in enumerate((-2, -1, 1, 2)):
        target = up(s, d)
        wanted = up(c - target, 1) < 3
        copy = remote(mrow, mall.at[2 - d], m_s.at[i], m_r.at[i], target, c)
        m_sends.append((wanted, copy))

        @pl.when(wanted)
        def _():
            copy.start()

    inside = jnp.where(active, 1.0, 0.0).astype(F32)

    def block(matrix):
        left, mid, right = (matrix[:, ROWS * i : ROWS * (i + 1)] for i in range(3))
        return jnp.where(e == 0, left, jnp.where(e == 1, mid, right)) * inside

    metric[...] = block(m_own)
    for a in range(ATOMS):
        ham[4 * a : 4 * a + 4, :] = block(ag[a, 4:8, :])

    for copy in kr_copies:
        copy.wait_recv()
    k0cat = split(jnp.concatenate([k0row[t] for t in range(n)], axis=1))
    for copy in b_copies:
        copy.wait_recv()
    bcol = split(ball[...].reshape(n * ROWS, ROWS))
    y_own = dot3(k0cat, bcol)
    y1[...] = y_own
    y_sends = []
    for i in range(3):
        target = up(s, i - 1)
        wanted = target != c
        copy = remote(y1, y1all.at[c], y_s.at[i], y_r.at[c], s, target)
        y_sends.append((wanted, copy))

        @pl.when(wanted)
        def _():
            copy.start()

    pur[...] = jnp.zeros((ROWS, ROWS), F32)

    @pl.when(active)
    def _():
        y1all[c] = y_own
        for k in range(1, n):
            other = up(c, k)
            remote(y1, y1all.at[other], y_s.at[0], y_r.at[other], s, other).wait_recv()
        ycat = split(jnp.concatenate([y1all[t] for t in range(n)], axis=1))
        first = mask[...] * (3.0 * y_own - 2.0 * dot3(ycat, bcol))
        k1[...] = first
        for i, (d, f) in enumerate(pairs):
            t, v = up(s, d), up(s, d + f - 1)

            @pl.when(jnp.logical_not((d == 0) & (v == c)))
            def _():
                remote(k1, k1all.at[(2 - d) * 3 + e], k_s.at[i], k_r.at[(2 - d) * 3 + e], t, v).start()

        k1all[6 + e] = first
        mall[2] = m_own
        for i, d in enumerate((-2, -1, 1, 2)):
            remote(mrow, mall.at[2 - d], m_s.at[i], m_r.at[i], up(s, d), c).wait_recv()
        for i, (d, f) in enumerate(pairs):
            t, v = up(s, d), up(s, d + f - 1)

            @pl.when(jnp.logical_not((d == 0) & (v == c)))
            def _():
                remote(k1, k1all.at[i], k_s.at[i], k_r.at[i], t, v).wait_recv()

        kb = {}
        mb = {}
        for r in range(5):
            mr = mall[r]
            for f in range(3):
                kb[r, r + f] = k1all[3 * r + f]
                mb[r, r + f] = mr[:, ROWS * f : ROWS * f + ROWS]
        zero = jnp.zeros((ROWS, ROWS), F32)

        def window(blocks, rows, cols):
            return jnp.concatenate(
                [jnp.concatenate([blocks.get((r, q), zero) for q in cols], axis=1) for r in rows], axis=0
            )

        k_window = window(kb, range(5), range(7))
        m_window = split(window(mb, range(5), range(7)))
        x2 = dot3(split(window(kb, [2], [2, 3, 4])), split(window(mb, [1, 2, 3], range(1, 6))))
        y2 = dot3(split(x2), split(k_window))
        w2 = dot3(split(y2), m_window, (((1,), (1,)), ((), ())))
        columns = [
            jnp.concatenate([kb.get((r, q), zero) for r in range(5)], axis=0) for q in (2, 3, 4)
        ]
        kcol = jnp.where(e == 0, columns[0], jnp.where(e == 1, columns[1], columns[2]))
        y2s = jnp.where(
            e == 0, y2[:, 2 * ROWS : 3 * ROWS], jnp.where(e == 1, y2[:, 3 * ROWS : 4 * ROWS], y2[:, 4 * ROWS : 5 * ROWS])
        )
        pur[...] = mask[...] * (3.0 * y2s - 2.0 * dot3(split(w2), split(kcol)))
        for i, (d, f) in enumerate(pairs):
            t, v = up(s, d), up(s, d + f - 1)

            @pl.when(jnp.logical_not((d == 0) & (v == c)))
            def _():
                remote(k1, k1all.at[(2 - d) * 3 + e], k_s.at[i], k_r.at[i], t, v).wait_send()

    for copy in rs_copies + kn_copies + kr_copies + ag_copies + b_copies:
        copy.wait_send()
    for wanted, copy in m_sends + y_sends:

        @pl.when(wanted)
        def _():
            copy.wait_send()


def purify(n, part, kernel, mask):
    vmem = pl.BlockSpec(memory_space=pltpu.VMEM)
    block = jax.ShapeDtypeStruct((ROWS, ROWS), F32)
    dma = pltpu.SemaphoreType.DMA
    return pl.pallas_call(
        functools.partial(purify_kernel, n),
        out_shape=(block, block, block),
        in_specs=[vmem] * 3,
        out_specs=(vmem, vmem, vmem),
        scratch_shapes=[
            pltpu.VMEM((n - 1, 8, 3 * ROWS), F32),
            pltpu.VMEM((8, 3 * ROWS), F32),
            pltpu.VMEM((n, 8, 3 * ROWS), F32),
            pltpu.VMEM((n, ROWS, ROWS), F32),
            pltpu.VMEM((2, ROWS, ROWS), F32),
            pltpu.VMEM((ROWS, ROWS), F32),
            pltpu.VMEM((n, ROWS, ROWS), F32),
            pltpu.VMEM((ROWS, ROWS), F32),
            pltpu.VMEM((n, ROWS, ROWS), F32),
            pltpu.VMEM((ROWS, ROWS), F32),
            pltpu.VMEM((15, ROWS, ROWS), F32),
            pltpu.VMEM((ROWS, 3 * ROWS), F32),
            pltpu.VMEM((5, ROWS, 3 * ROWS), F32),
            dma((n,)), dma((n,)), dma((n,)), dma((n,)), dma((n,)), dma((n,)),
            dma((2,)), dma((2,)), dma((n,)), dma((n,)), dma((3,)), dma((n,)),
            dma((15,)), dma((15,)), dma((4,)), dma((4,)),
        ],
        compiler_params=pltpu.CompilerParams(
            collective_id=0, has_side_effects=True, vmem_limit_bytes=32 * 1024 * 1024
        ),
    )(part, kernel, mask)


def local(supports, potential, anchors, kernel):
    slab = lax.axis_index("atoms")
    col = lax.axis_index("cols")
    slabs = lax.axis_size("atoms")
    cols = lax.axis_size("cols")
    x = supports.transpose(2, 3, 0, 1, 4).reshape(27, ROWS, 256)
    v = potential.transpose(1, 2, 0, 3).reshape(27, ATOMS, 256)
    ring = [(i, (i + 1) % cols) for i in range(cols)]
    back = [(j, i) for i, j in ring]
    line = [(i, i + 1) for i in range(slabs - 1)]
    line_back = [(j, i) for i, j in line]
    lo = lax.ppermute(x, "cols", ring)
    hi = lax.ppermute(x, "cols", back)
    bl = lax.ppermute(x[9:], "atoms", line)
    bu = lax.ppermute(x[:18], "atoms", line_back)

    far = jnp.full((ATOMS, 3), -100, jnp.int32)
    padded = jnp.concatenate([far, anchors, -2 * far], axis=0)
    band = lax.dynamic_slice_in_dim(padded, slab * ATOMS, 3 * ATOMS, 0)
    corner = (band[:, 0] - 3 * slab) * 36 + band[:, 1] * 6 + band[:, 2]
    flags = jnp.stack([col == 0, col == cols - 1]).astype(jnp.int32)
    scalars = jnp.concatenate([corner[ATOMS : 2 * ATOMS], corner[:ATOMS], corner[2 * ATOMS :], flags])
    part = gram(scalars, x, lo, hi, bl, bu, v)

    rows = lax.dynamic_slice_in_dim(anchors, slab * ATOMS, ATOMS, 0)
    columns = lax.dynamic_slice_in_dim(anchors, col * ATOMS, ATOMS, 0)
    near = jnp.all(jnp.abs(columns[None] - rows[:, None]) <= 2, axis=-1).astype(F32)
    mask = jnp.broadcast_to(near[:, None, :, None], (ATOMS, FUNCS, ATOMS, FUNCS)).reshape(ROWS, ROWS)
    return purify(slabs, part, kernel, mask)


def solution(mesh):
    in_specs = (
        P("atoms", None, None, "cols", None),
        P("atoms", None, "cols", None),
        P(),
        P("atoms", "cols"),
    )
    out_specs = (P("atoms", "cols"), P("atoms", "cols"), P("atoms", "cols"))
    return jax.shard_map(local, mesh=mesh, in_specs=in_specs, out_specs=out_specs, check_vma=False)
```

profile of v0, /device:TPU:1, one launch (start us, length us, event | category | flops | bytes accessed | tf_op | source)
XLA Modules:
  0.0 110.8 jit_solution(17995530081735205466)
XLA Ops:
  0.6 1.6 %copy.19 = bf16[27,1,16,4,256]{4,3,2,0,1:T(4,128)(2,1)S(1)} copy(bf16[27,1,16,4,256]{4,3,1,0,2:T(4,128)(2,1)} %bitcast.22) | data formatting | bytes 1769472 | tf_op jit(solution)/shard_map/transpose | solution.py:377
  2.3 0.0 copy-start.2
  2.3 0.2 reshape.33.x_ref
  2.5 3.0 %collective-permute-start = (bf16[27,64,256]{2,1,0:T(8,128)(2,1)S(1)}, bf16[27,64,256]{2,1,0:T(8,128)(2,1)S(1)}, u32[]{:S(2)}, u32[]{:S(2)}) collective-permute-start(bf16[27,64,256]{2,1,0:T(8,128)(2,1)S(1)} %reshape.33.x_ref), channel_id=1, source_target_pairs={{0,1},{1,2},{2,3},{3,4},{4,5},{5,6},{6,7},{7,8},{8,9},{9,10},{10,1... | collective-permute-start | bytes 2654216 | tf_op jit(solution)/shard_map/ppermute | solution.py:383
  5.5 0.2 collective-permute-start.1
  5.7 0.4 fusion.3
  6.1 0.3 copy.20
  6.4 0.1 slice.49
  6.6 3.8 %collective-permute-start.2 = (bf16[18,64,256]{2,1,0:T(8,128)(2,1)S(1)}, bf16[18,64,256]{2,1,0:T(8,128)(2,1)}, u32[]{:S(2)}, u32[]{:S(2)}) collective-permute-start(bf16[18,64,256]{2,1,0:T(8,128)(2,1)S(1)} %slice.49), channel_id=1, source_target_pairs={{0,16},{16,32},{32,48},{48,64},{64,80},{80,96},{96,112},{112,128},... | collective-permute-start | bytes 1769480 | tf_op jit(solution)/shard_map/ppermute | solution.py:385
  10.4 0.3 copy.21
  10.7 1.0 slice.51
  11.6 1.3 %collective-permute-start.3 = (bf16[18,64,256]{2,1,0:T(8,128)(2,1)}, bf16[18,64,256]{2,1,0:T(8,128)(2,1)S(1)}, u32[]{:S(2)}, u32[]{:S(2)}) collective-permute-start(bf16[18,64,256]{2,1,0:T(8,128)(2,1)} %slice.51), channel_id=1, source_target_pairs={{16,0},{32,16},{48,32},{64,48},{80,64},{96,80},{112,96},{128,112},... | collective-permute-start | bytes 1769480 | tf_op jit(solution)/shard_map/ppermute | solution.py:386
  13.0 0.7 copy-done.6
  13.6 0.1 constant_dynamic-slice_fusion.1
  13.7 0.1 fusion
  13.8 0.1 pad_dynamic-slice_fusion.1
  13.9 0.1 fusion.2
  14.0 0.1 add_convert_fusion
  14.1 0.1 broadcast_in_dim.5
  14.2 0.3 reshape.35.mask
  14.4 0.1 slice_bitcast_fusion.2
  14.5 0.6 pad_add_fusion.sc
  15.1 3.4 %collective-permute-done.2.bl_ref = bf16[18,64,256]{2,1,0:T(8,128)(2,1)} collective-permute-done((bf16[18,64,256]{2,1,0:T(8,128)(2,1)S(1)}, bf16[18,64,256]{2,1,0:T(8,128)(2,1)}, u32[]{:S(2)}, u32[]{:S(2)}) %collective-permute-start.2) | collective-permute-done | bytes 589856 | tf_op jit(solution)/shard_map/ppermute | solution.py:385
  18.5 6.1 %collective-permute-done.3.bu_ref = bf16[18,64,256]{2,1,0:T(8,128)(2,1)S(1)} collective-permute-done((bf16[18,64,256]{2,1,0:T(8,128)(2,1)}, bf16[18,64,256]{2,1,0:T(8,128)(2,1)S(1)}, u32[]{:S(2)}, u32[]{:S(2)}) %collective-permute-start.3) | collective-permute-done | bytes 589856 | tf_op jit(solution)/shard_map/ppermute | solution.py:386
  24.6 0.8 copy-done.5
  25.4 0.3 copy-done.4
  25.7 18.3 %shard_map.67.part = f32[16,8,192]{2,1,0:T(8,128)} custom-call(s32[50]{0:T(128)} %pad_add_fusion.sc, bf16[27,64,256]{2,1,0:T(8,128)(2,1)} %copy-done.3, bf16[27,64,256]{2,1,0:T(8,128)(2,1)} %copy-done.4, bf16[27,64,256]{2,1,0:T(8,128)(2,1)} %collective-permute-done.1.hi_ref, bf16[18,64,256]{2,1,0:T(8,128)(2,1)} %collective-permute-done.2.bl_ref, ...), custom_call_target="tpu_custom_call" | custom-call | tf_op jit(solution)/shard_map/pallas_call | solution.py:132
  44.0 0.9 copy-done
  44.9 64.0 %shard_map.68 = (f32[64,64]{1,0:T(8,128)S(1)}, f32[64,64]{1,0:T(8,128)S(1)}, f32[64,64]{1,0:T(8,128)S(1)}) custom-call(f32[16,8,192]{2,1,0:T(8,128)S(1)} %copy-done, f32[64,64]{1,0:T(8,128)S(1)} %copy-done.1, f32[64,64]{1,0:T(8,128)S(1)} %reshape.35.mask), custom_call_target="tpu_custom_call" | custom-call | tf_op jit(solution)/shard_map/pallas_call | solution.py:343
  108.9 0.6 copy.26
  109.6 0.6 copy.27
  110.2 0.6 copy.28
  (15 shorter events, 0.0 us)
Async XLA Ops:
  2.3 3.5 %copy-start.2 = (bf16[16,4,27,1,256]{4,1,3,2,0:T(4,128)(2,1)S(1)}, bf16[16,4,27,1,256]{4,1,3,2,0:T(4,128)(2,1)}, u32[]{:S(2)}) copy-start(bf16[16,4,27,1,256]{4,1,3,2,0:T(4,128)(2,1)} %param.4) | copy-start | bytes 2654212
  2.5 3.7 %copy-start.3 = (bf16[27,64,256]{2,1,0:T(8,128)(2,1)}, bf16[27,64,256]{2,1,0:T(8,128)(2,1)S(1)}, u32[]{:S(2)}) copy-start(bf16[27,64,256]{2,1,0:T(8,128)(2,1)S(1)} %reshape.33.x_ref) | copy-start | bytes 2654212
  2.5 22.1 %collective-permute-start = (bf16[27,64,256]{2,1,0:T(8,128)(2,1)S(1)}, bf16[27,64,256]{2,1,0:T(8,128)(2,1)S(1)}, u32[]{:S(2)}, u32[]{:S(2)}) collective-permute-start(bf16[27,64,256]{2,1,0:T(8,128)(2,1)S(1)} %reshape.33.x_ref), channel_id=1, source_target_pairs={{0,1},{1,2},{2,3},{3,4},{4,5},{5,6},{6,7},{7,8},{8,9},{9,10},{10,1... | collective-permute-start | bytes 2654216 | tf_op jit(solution)/shard_map/ppermute | solution.py:383
  5.5 19.0 %collective-permute-start.1 = (bf16[27,64,256]{2,1,0:T(8,128)(2,1)S(1)}, bf16[27,64,256]{2,1,0:T(8,128)(2,1)}, u32[]{:S(2)}, u32[]{:S(2)}) collective-permute-start(bf16[27,64,256]{2,1,0:T(8,128)(2,1)S(1)} %reshape.33.x_ref), channel_id=1, source_target_pairs={{1,0},{2,1},{3,2},{4,3},{5,4},{6,5},{7,6},{8,7},{9,8},{10,9},{11,1... | collective-permute-start | bytes 2654216 | tf_op jit(solution)/shard_map/ppermute | solution.py:384
  6.6 11.9 %collective-permute-start.2 = (bf16[18,64,256]{2,1,0:T(8,128)(2,1)S(1)}, bf16[18,64,256]{2,1,0:T(8,128)(2,1)}, u32[]{:S(2)}, u32[]{:S(2)}) collective-permute-start(bf16[18,64,256]{2,1,0:T(8,128)(2,1)S(1)} %slice.49), channel_id=1, source_target_pairs={{0,16},{16,32},{32,48},{48,64},{64,80},{80,96},{96,112},{112,128},... | collective-permute-start | bytes 1769480 | tf_op jit(solution)/shard_map/ppermute | solution.py:385
  11.6 12.9 %collective-permute-start.3 = (bf16[18,64,256]{2,1,0:T(8,128)(2,1)}, bf16[18,64,256]{2,1,0:T(8,128)(2,1)S(1)}, u32[]{:S(2)}, u32[]{:S(2)}) collective-permute-start(bf16[18,64,256]{2,1,0:T(8,128)(2,1)} %slice.51), channel_id=1, source_target_pairs={{16,0},{32,16},{48,32},{64,48},{80,64},{96,80},{112,96},{128,112},... | collective-permute-start | bytes 1769480 | tf_op jit(solution)/shard_map/ppermute | solution.py:386
  12.9 0.7 copy-start.6
  24.5 0.8 copy-start.5
  24.6 1.1 %copy-start.4 = (bf16[27,64,256]{2,1,0:T(8,128)(2,1)}, bf16[27,64,256]{2,1,0:T(8,128)(2,1)S(1)}, u32[]{:S(2)}) copy-start(bf16[27,64,256]{2,1,0:T(8,128)(2,1)S(1)} %collective-permute-done.lo_ref) | copy-start | bytes 2654212
  25.7 18.3 %copy-start.1 = (f32[64,64]{1,0:T(8,128)S(1)}, f32[64,64]{1,0:T(8,128)}, u32[]{:S(2)}) copy-start(f32[64,64]{1,0:T(8,128)} %k0.1) | copy-start | bytes 49156
  44.0 0.9 copy-start
where the time goes:
time: 111 us
  Pallas kernels  82.4 us (74%)
  waiting for transfers between devices  9.45 us (9%)
  local copies, waits for them, and re-layouts  9.02 us (8%)
  starting transfers between devices  8.34 us (8%)
    pallas_call x1, Pallas kernels, purify(): pl.pallas_call(functools.partial(purify_kernel, n), out_shape=(block, blo...  64 us
    pallas_call x1, Pallas kernels, gram(): pl.pallas_call(gram_kernel, out_shape=jax.ShapeDtypeStruct((ATOMS, 8, 3 *...  18.3 us
    ppermute x1, waiting for transfers between devices, local(): bu = lax.ppermute(x[:18], 'atoms', line_back)  6.09 us
    unnamed x17, local copies, waits for them, and re-layouts  4.55 us
    ppermute x1, starting transfers between devices, local(): bl = lax.ppermute(x[9:], 'atoms', line)  3.82 us
    ppermute x1, waiting for transfers between devices, local(): bl = lax.ppermute(x[9:], 'atoms', line)  3.35 us
    ppermute x1, starting transfers between devices, local(): lo = lax.ppermute(x, 'cols', ring)  3.03 us
  transfers between devices with their start and end apart: 4, of which 2 were waited for; matrix products, arithmetic and copies ran while one was open for 3% of the time, Pallas kernels for 0%

commit v1 on v0

v1 whole, which is shorter than its diff:
```python
import functools

import jax
import jax.numpy as jnp
from jax import lax
from jax.experimental import pallas as pl
from jax.experimental.pallas import tpu as pltpu
from jax.sharding import PartitionSpec as P

MESH = pl.DeviceIdType.MESH
F32 = jnp.float32
BF16 = jnp.bfloat16
GRID_BLOCKS = 180
ATOMS = 16
FUNCS = 4
ROWS = ATOMS * FUNCS


def split(a):
    high = a.astype(BF16)
    return high, (a - high.astype(F32)).astype(BF16)


def dot3(left, right, dims=(((1,), (0,)), ((), ()))):
    lh, ll = left
    rh, rl = right
    mm = functools.partial(lax.dot_general, dimension_numbers=dims, preferred_element_type=F32)
    return mm(lh, rh) + (mm(lh, rl) + mm(ll, rh))


def shift_matrices():
    source = lax.broadcasted_iota(jnp.int32, (256, 256), 0)
    target = lax.broadcasted_iota(jnp.int32, (256, 256), 1)
    step = target - source
    z = target % 16
    one = jnp.float32(1.0)
    own = jnp.where(step == 0, -6.0, 0.0)
    own = own + jnp.where((step == 1) & (z != 0), one, 0.0)
    own = own + jnp.where((step == -1) & (z != 15), one, 0.0)
    own = own + jnp.where((step == 16) | (step == -16), one, 0.0)
    z_low = jnp.where((step == -15) & (z == 0), one, 0.0)
    z_high = jnp.where((step == 15) & (z == 15), one, 0.0)
    y_low = jnp.where(step == -240, one, 0.0)
    y_high = jnp.where(step == 240, one, 0.0)
    return [m.astype(BF16) for m in (own, z_low, z_high, y_low, y_high)]


def mm(a, b):
    return jnp.dot(a, b, preferred_element_type=F32)


def remote(src, dst, ss, rs, row, col):
    return pltpu.make_async_remote_copy(
        src_ref=src, dst_ref=dst, send_sem=ss, recv_sem=rs, device_id=(row, col), device_id_type=MESH
    )


def signal_barrier(row, col):
    pl.semaphore_signal(
        pltpu.get_barrier_semaphore(), inc=1, device_id=(row, col), device_id_type=MESH
    )


def exchange_kernel(n, x_ref, v_ref, phi, hphi, bl, bu, lo, hi, base, send, recv):
    s = lax.axis_index("atoms")
    c = lax.axis_index("cols")
    up = lambda at, k: lax.rem(at + k + n, n)
    for d in (1, -1):
        signal_barrier(s, up(c, d))
        signal_barrier(up(s, d), c)
    pl.semaphore_wait(pltpu.get_barrier_semaphore(), 4)
    copies = [
        remote(x_ref.at[9:27], bl.at[0:18], send.at[0], recv.at[0], up(s, 1), c),
        remote(x_ref.at[0:18], bu.at[0:18], send.at[1], recv.at[1], up(s, -1), c),
        remote(x_ref, lo, send.at[2], recv.at[2], s, up(c, 1)),
        remote(x_ref, hi, send.at[3], recv.at[3], s, up(c, -1)),
    ]
    for copy in copies:
        copy.start()
    empty = jnp.zeros((ROWS, 256), BF16)
    phi[27] = empty
    hphi[27] = empty
    bl[18] = empty
    bu[18] = empty
    phi[0:27] = x_ref[...]
    own, z_low, z_high, y_low, y_high = shift_matrices()
    for bx in range(3):
        first = 9 * bx
        rows = lambda at, count: x_ref[first + at : first + at + count].reshape(count * ROWS, 256)
        base[first : first + 9] = mm(rows(0, 9), own).reshape(9, ROWS, 256)
        for by in range(3):
            f = 3 * by
            base[first + f + 1 : first + f + 3] += mm(rows(f, 2), z_low).reshape(2, ROWS, 256)
            base[first + f : first + f + 2] += mm(rows(f + 1, 2), z_high).reshape(2, ROWS, 256)
        base[first + 3 : first + 9] += mm(rows(0, 6), y_low).reshape(6, ROWS, 256)
        base[first : first + 6] += mm(rows(3, 6), y_high).reshape(6, ROWS, 256)
    pick = (
        lax.broadcasted_iota(jnp.int32, (ROWS, ATOMS), 0) // FUNCS
        == lax.broadcasted_iota(jnp.int32, (ROWS, ATOMS), 1)
    ).astype(F32).astype(BF16)
    for p in range(27):
        base[p] = -0.5 * base[p] + mm(pick, v_ref[p]) * x_ref[p].astype(F32)
    copies[2].wait_recv()
    copies[3].wait_recv()
    first = jnp.where(c == 0, 1, 0)
    last = jnp.where(c == n - 1, 1, 0)
    for p in range(27):
        if p < 9:
            low = lo[p].astype(F32) * (1 - first).astype(F32)
        else:
            low = lo[p - 9 * first].astype(F32)
        if p >= 18:
            high = hi[p].astype(F32) * (1 - last).astype(F32)
        else:
            high = hi[p + 9 * last].astype(F32)
        hphi[p] = (base[p] - 0.5 * (low + high)).astype(BF16)
    copies[0].wait_recv()
    copies[1].wait_recv()
    for copy in copies:
        copy.wait_send()


def exchange(n, x, v):
    vmem = pl.BlockSpec(memory_space=pltpu.VMEM)
    blocks = lambda count: jax.ShapeDtypeStruct((count, ROWS, 256), BF16)
    return pl.pallas_call(
        functools.partial(exchange_kernel, n),
        out_shape=(blocks(28), blocks(28), blocks(19), blocks(19)),
        in_specs=[vmem] * 2,
        out_specs=(vmem,) * 4,
        scratch_shapes=[
            pltpu.VMEM((27, ROWS, 256), BF16),
            pltpu.VMEM((27, ROWS, 256), BF16),
            pltpu.VMEM((27, ROWS, 256), F32),
            pltpu.SemaphoreType.DMA((4,)),
            pltpu.SemaphoreType.DMA((4,)),
        ],
        compiler_params=pltpu.CompilerParams(
            collective_id=1, has_side_effects=True, vmem_limit_bytes=32 * 1024 * 1024
        ),
    )(x, v)


def pack(block):
    return jnp.concatenate([block[: ROWS // 2], block[ROWS // 2 :]], axis=1)


def unpack(packed):
    return jnp.concatenate([packed[:, :ROWS], packed[:, ROWS:]], axis=0)


def side_by_side(ref, n):
    lane = lax.broadcasted_iota(jnp.int32, (ROWS // 2, 2 * ROWS), 1) < ROWS
    tiles = []
    for t in range(0, n, 2):
        even, odd = ref[t], ref[t + 1]
        top = jnp.where(lane, even, pltpu.roll(odd, ROWS, 1))
        low = jnp.where(lane, pltpu.roll(even, ROWS, 1), odd)
        tiles.append(jnp.concatenate([top, low], axis=0))
    return jnp.concatenate(tiles, axis=1)


def stacked(ref, n):
    return jnp.concatenate([unpack(ref[t]) for t in range(n)], axis=0)


def gram_pass(table, phi, hphi, band, row, start, count, batch):
    def gather(ref, at, shift):
        tiles = []
        for i in range(4):
            picked = [
                ref[table[at + shift + 4 * i + j], 16 * i : 16 * i + 16, :] for j in range(4)
            ]
            tiles.append(
                jnp.where(
                    row < 8,
                    jnp.where(row < 4, picked[0], picked[1]),
                    jnp.where(row < 12, picked[2], picked[3]),
                )
            )
        return jnp.concatenate(tiles, axis=0)

    columns = ROWS if band is None else 2 * ROWS

    def step(i, acc):
        left, right = [], []
        for k in range(batch):
            at = (start + batch * i + k) * 32
            values = gather(phi, at, 0)
            left.append(jnp.concatenate([gather(hphi, at, 0), values], axis=0))
            if band is None:
                right.append(values)
            else:
                right.append(jnp.concatenate([values, gather(band, at, 16)], axis=0))
        left = jnp.concatenate(left, axis=1)
        right = jnp.concatenate(right, axis=1)
        return acc + lax.dot_general(left, right, (((1,), (1,)), ((), ())), preferred_element_type=F32)

    return lax.fori_loop(0, count // batch, step, jnp.zeros((2 * ROWS, columns), F32))


def purify_kernel(
    n, table, phi, hphi, bl, bu, k0, mask, out,
    part, k0p, rs_buf, piece, ag, k0row, k0n, bblk, ball, y1, y1all, k1, k1all, mrow, mall,
    rs_s, rs_r, ag_s, ag_r, kr_s, kr_r, kn_s, kn_r, b_s, b_r, y_s, y_r, k_s, k_r, m_s, m_r,
):
    s = lax.axis_index("atoms")
    c = lax.axis_index("cols")
    up = lambda base, k: lax.rem(base + k + 2 * n, n)
    e = up(c - s, 1)
    active = e < 3

    for k in range(1, n):
        signal_barrier(s, up(c, k))
        signal_barrier(up(s, k), c)
    pairs = [(d, f) for d in range(-2, 3) for f in range(3)]
    k0p[...] = pack(k0[...])
    row = lax.broadcasted_iota(jnp.int32, (16, 256), 0).astype(F32).astype(BF16)
    lower = gram_pass(table, phi, hphi, bl, row, 0, 72, 4)
    pl.semaphore_wait(pltpu.get_barrier_semaphore(), 2 * (n - 1))
    kn_copies = []
    for i, d in enumerate((1, -1)):
        copy = remote(k0p, k0n.at[i], kn_s.at[i], kn_r.at[i], up(s, d), c)
        copy.start()
        kn_copies.append(copy)
    kr_copies = []
    for k in range(1, n):
        copy = remote(k0p, k0row.at[c], kr_s.at[k - 1], kr_r.at[k - 1], s, up(c, k))
        copy.start()
        kr_copies.append(copy)
    k0row[c] = k0p[...]
    middle = gram_pass(table, phi, hphi, None, row, 72, 36, 4)
    upper = gram_pass(table, phi, hphi, bu, row, 108, 72, 4)
    sums = jnp.concatenate(
        [lower[:, ROWS:], lower[:, :ROWS] + middle + upper[:, :ROWS], upper[:, ROWS:]], axis=1
    )
    for a in range(ATOMS):
        part[a, 0:4, :] = sums[ROWS + 4 * a : ROWS + 4 * a + 4, :]
        part[a, 4:8, :] = sums[4 * a : 4 * a + 4, :]

    rs_copies = []
    for k in range(1, n):
        col = up(c, k)
        copy = remote(part.at[col], rs_buf.at[k - 1], rs_s.at[k - 1], rs_r.at[k - 1], s, col)
        copy.start()
        rs_copies.append(copy)
    total = part[c]
    for k in range(1, n):
        rs_copies[k - 1].wait_recv()
        total = total + rs_buf[k - 1]
    piece[...] = total
    ag[c] = total
    ag_copies = []
    for k in range(1, n):
        copy = remote(piece, ag.at[c], ag_s.at[k - 1], ag_r.at[k - 1], s, up(c, k))
        copy.start()
        ag_copies.append(copy)
    for copy in kn_copies:
        copy.wait_recv()
    panel = split(jnp.concatenate([unpack(k0n[0]), k0[...], unpack(k0n[1])], axis=0))
    for copy in ag_copies:
        copy.wait_recv()
    for a in range(ATOMS):
        mrow[4 * a : 4 * a + 4, :] = ag[a, 0:4, :]
    m_own = mrow[...]
    bblk[...] = pack(dot3(split(m_own), panel))
    b_copies = []
    for k in range(1, n):
        copy = remote(bblk, ball.at[s], b_s.at[k - 1], b_r.at[k - 1], up(s, k), c)
        copy.start()
        b_copies.append(copy)
    ball[s] = bblk[...]
    m_sends = []
    for i, d in enumerate((-2, -1, 1, 2)):
        target = up(s, d)
        wanted = up(c - target, 1) < 3
        copy = remote(mrow, mall.at[2 - d], m_s.at[i], m_r.at[i], target, c)
        m_sends.append((wanted, copy))

        @pl.when(wanted)
        def _():
            copy.start()

    inside = jnp.where(active, 1.0, 0.0).astype(F32)

    def block(matrix):
        left, mid, right = (matrix[:, ROWS * i : ROWS * (i + 1)] for i in range(3))
        return jnp.where(e == 0, left, jnp.where(e == 1, mid, right)) * inside

    out[0] = block(m_own)
    for a in range(ATOMS):
        out[1, 4 * a : 4 * a + 4, :] = block(ag[a, 4:8, :])

    for copy in kr_copies:
        copy.wait_recv()
    k0cat = split(side_by_side(k0row, n))
    for copy in b_copies:
        copy.wait_recv()
    bcol = split(stacked(ball, n))
    y_own = dot3(k0cat, bcol)
    y1[...] = pack(y_own)
    y_sends = []
    for i in range(3):
        target = up(s, i - 1)
        wanted = target != c
        copy = remote(y1, y1all.at[c], y_s.at[i], y_r.at[c], s, target)
        y_sends.append((wanted, copy))

        @pl.when(wanted)
        def _():
            copy.start()

    out[2] = jnp.zeros((ROWS, ROWS), F32)

    @pl.when(active)
    def _():
        y1all[c] = y1[...]
        for k in range(1, n):
            other = up(c, k)
            remote(y1, y1all.at[other], y_s.at[0], y_r.at[other], s, other).wait_recv()
        ycat = split(side_by_side(y1all, n))
        first = mask[...] * (3.0 * y_own - 2.0 * dot3(ycat, bcol))
        k1[...] = pack(first)
        for i, (d, f) in enumerate(pairs):
            t, v = up(s, d), up(s, d + f - 1)

            @pl.when(jnp.logical_not((d == 0) & (v == c)))
            def _():
                remote(k1, k1all.at[(2 - d) * 3 + e], k_s.at[i], k_r.at[(2 - d) * 3 + e], t, v).start()

        k1all[6 + e] = k1[...]
        mall[2] = m_own
        for i, d in enumerate((-2, -1, 1, 2)):
            remote(mrow, mall.at[2 - d], m_s.at[i], m_r.at[i], up(s, d), c).wait_recv()
        for i, (d, f) in enumerate(pairs):
            t, v = up(s, d), up(s, d + f - 1)

            @pl.when(jnp.logical_not((d == 0) & (v == c)))
            def _():
                remote(k1, k1all.at[i], k_s.at[i], k_r.at[i], t, v).wait_recv()

        kb = {}
        mb = {}
        for r in range(5):
            mr = mall[r]
            for f in range(3):
                kb[r, r + f] = unpack(k1all[3 * r + f])
                mb[r, r + f] = mr[:, ROWS * f : ROWS * f + ROWS]
        zero = jnp.zeros((ROWS, ROWS), F32)

        def window(blocks, rows, cols):
            return jnp.concatenate(
                [jnp.concatenate([blocks.get((r, q), zero) for q in cols], axis=1) for r in rows], axis=0
            )

        k_window = window(kb, range(5), range(7))
        m_window = split(window(mb, range(5), range(7)))
        x2 = dot3(split(window(kb, [2], [2, 3, 4])), split(window(mb, [1, 2, 3], range(1, 6))))
        y2 = dot3(split(x2), split(k_window))
        w2 = dot3(split(y2), m_window, (((1,), (1,)), ((), ())))
        columns = [
            jnp.concatenate([kb.get((r, q), zero) for r in range(5)], axis=0) for q in (2, 3, 4)
        ]
        kcol = jnp.where(e == 0, columns[0], jnp.where(e == 1, columns[1], columns[2]))
        y2s = jnp.where(
            e == 0, y2[:, 2 * ROWS : 3 * ROWS], jnp.where(e == 1, y2[:, 3 * ROWS : 4 * ROWS], y2[:, 4 * ROWS : 5 * ROWS])
        )
        out[2] = mask[...] * (3.0 * y2s - 2.0 * dot3(split(w2), split(kcol)))
        for i, (d, f) in enumerate(pairs):
            t, v = up(s, d), up(s, d + f - 1)

            @pl.when(jnp.logical_not((d == 0) & (v == c)))
            def _():
                remote(k1, k1all.at[(2 - d) * 3 + e], k_s.at[i], k_r.at[i], t, v).wait_send()

    for copy in rs_copies + kn_copies + kr_copies + ag_copies + b_copies:
        copy.wait_send()
    for wanted, copy in m_sends + y_sends:

        @pl.when(wanted)
        def _():
            copy.wait_send()


def purify(n, table, phi, hphi, bl, bu, kernel, mask):
    vmem = pl.BlockSpec(memory_space=pltpu.VMEM)
    dma = pltpu.SemaphoreType.DMA
    half = lambda *lead: pltpu.VMEM((*lead, ROWS // 2, 2 * ROWS), F32)
    return pl.pallas_call(
        functools.partial(purify_kernel, n),
        out_shape=jax.ShapeDtypeStruct((3, ROWS, ROWS), F32),
        in_specs=[pl.BlockSpec(memory_space=pltpu.SMEM)] + [vmem] * 6,
        out_specs=vmem,
        scratch_shapes=[
            pltpu.VMEM((n, 8, 3 * ROWS), F32),
            half(),
            pltpu.VMEM((n - 1, 8, 3 * ROWS), F32),
            pltpu.VMEM((8, 3 * ROWS), F32),
            pltpu.VMEM((n, 8, 3 * ROWS), F32),
            half(n),
            half(2),
            half(),
            half(n),
            half(),
            half(n),
            half(),
            half(15),
            pltpu.VMEM((ROWS, 3 * ROWS), F32),
            pltpu.VMEM((5, ROWS, 3 * ROWS), F32),
            dma((n,)), dma((n,)), dma((n,)), dma((n,)), dma((n,)), dma((n,)),
            dma((2,)), dma((2,)), dma((n,)), dma((n,)), dma((3,)), dma((n,)),
            dma((15,)), dma((15,)), dma((4,)), dma((4,)),
        ],
        compiler_params=pltpu.CompilerParams(
            collective_id=0, has_side_effects=True, vmem_limit_bytes=40 * 1024 * 1024
        ),
    )(table, phi, hphi, bl, bu, kernel, mask)


def block_table(band, slab):
    blocks = jnp.arange(GRID_BLOCKS, dtype=jnp.int32)
    place = jnp.stack([blocks // 36 + 3 * slab, blocks // 6 % 6, blocks % 6], axis=-1)
    offset = place[:, None, :] - band[None, :, :]
    inside = jnp.all((offset >= 0) & (offset <= 2), axis=-1)
    index = offset[..., 0] * 9 + offset[..., 1] * 3 + offset[..., 2]
    own = jnp.where(inside, index, 27)[:, ATOMS : 2 * ATOMS]
    lower = jnp.where(inside, index - 9, 18)[:, :ATOMS]
    upper = jnp.where(inside, index, 18)[:, 2 * ATOMS :]
    other = jnp.where(blocks[:, None] < 72, lower, upper)
    return jnp.concatenate([own, other], axis=1).reshape(-1)


def local(supports, potential, anchors, kernel):
    slab = lax.axis_index("atoms")
    col = lax.axis_index("cols")
    slabs = lax.axis_size("atoms")
    x = supports.transpose(2, 3, 0, 1, 4).reshape(27, ROWS, 256)
    v = potential.transpose(1, 2, 0, 3).reshape(27, ATOMS, 256)
    phi, hphi, bl, bu = exchange(slabs, x, v)
    far = jnp.full((ATOMS, 3), -100, jnp.int32)
    padded = jnp.concatenate([far, anchors, -2 * far], axis=0)
    band = lax.dynamic_slice_in_dim(padded, slab * ATOMS, 3 * ATOMS, 0)
    table = block_table(band, slab)
    rows = lax.dynamic_slice_in_dim(anchors, slab * ATOMS, ATOMS, 0)
    columns = lax.dynamic_slice_in_dim(anchors, col * ATOMS, ATOMS, 0)
    near = jnp.all(jnp.abs(columns[None] - rows[:, None]) <= 2, axis=-1).astype(F32)
    mask = jnp.broadcast_to(near[:, None, :, None], (ATOMS, FUNCS, ATOMS, FUNCS)).reshape(ROWS, ROWS)
    out = purify(slabs, table, phi, hphi, bl, bu, kernel, mask)
    return out[0], out[1], out[2]


def solution(mesh):
    in_specs = (
        P("atoms", None, None, "cols", None),
        P("atoms", None, "cols", None),
        P(),
        P("atoms", "cols"),
    )
    out_specs = (P("atoms", "cols"), P("atoms", "cols"), P("atoms", "cols"))
    return jax.shard_map(local, mesh=mesh, in_specs=in_specs, out_specs=out_specs, check_vma=False)
```

time: 111 us -> 84.3 us (0.76)
  waiting for transfers between devices: 9.45 us -> 0 us
  starting transfers between devices: 8.34 us -> 0 us
  Pallas kernels: 82.4 us -> 75.6 us
  local copies, waits for them, and re-layouts: 9.02 us -> 7.31 us
    ppermute x4 -> x0, waiting for transfers between devices: 9.45 us -> none  [the longest x1 6.09 us: local(): bu = lax.ppermute(x[:18], 'atoms', line_back)]
    ppermute x4 -> x0, starting transfers between devices: 8.34 us -> none  [the longest x1 3.82 us: local(): bl = lax.ppermute(x[9:], 'atoms', line)]
    pallas_call x2, Pallas kernels: 82.4 us -> 75.6 us  [the longest x1 55.9 us: purify(): pl.pallas_call(functools.partial(purify_kernel, n), out_shape=jax.ShapeDt...]
    unnamed x17 -> x10, local copies, waits for them, and re-layouts: 4.55 us -> 2.34 us
    slice x6 -> x0, local copies, waits for them, and re-layouts: 2.13 us -> none  [the longest x3 1.64 us: local(): bu = lax.ppermute(x[:18], 'atoms', line_back)]
  transfers between devices with their start and end apart: 4 -> 0, of which waited for: 2 -> 0; matrix products, arithmetic and copies ran while one was open for 3% -> 0% of each run, Pallas kernels for 0% -> 0%
where the time goes in v1:
time: 84.3 us; the launch traced here: 84.1 us
  Pallas kernels  75.6 us (90%)
  local copies, waits for them, and re-layouts  7.31 us (9%)
    pallas_call x1, Pallas kernels, purify(): pl.pallas_call(functools.partial(purify_kernel, n), out_shape=jax.ShapeDt...  55.9 us
    pallas_call x1, Pallas kernels, exchange(): pl.pallas_call(functools.partial(exchange_kernel, n), out_shape=(blocks(2...  19.7 us
    unnamed x10, local copies, waits for them, and re-layouts  2.34 us

profile of v1, /device:TPU:1, one launch (start us, length us, event | category | flops | bytes accessed | tf_op | source)
XLA Modules:
  0.0 84.1 jit_solution(10242972295024329253)
XLA Ops:
  0.6 0.0 copy-start.4
  0.7 0.1 pad_dynamic-slice_fusion.1
  0.8 0.6 copy-done.4
  1.3 0.1 fusion.6
  1.5 0.1 broadcast_subtract_fusion
  1.6 0.1 and_reduce_fusion
  1.7 0.1 copy.17
  1.8 0.1 reshape.129.table
  1.9 1.6 %copy.18 = bf16[27,1,16,4,256]{4,3,2,0,1:T(4,128)(2,1)S(1)} copy(bf16[27,1,16,4,256]{4,3,1,0,2:T(4,128)(2,1)} %bitcast.19) | data formatting | bytes 1769472 | tf_op jit(solution)/shard_map/transpose | solution.py:437
  3.6 0.2 reshape.130.x_ref
  3.8 0.0 copy-start.2
  3.8 0.9 %copy-done.2 = bf16[16,27,1,256]{3,0,2,1:T(8,128)(2,1)S(1)} copy-done((bf16[16,27,1,256]{3,0,2,1:T(8,128)(2,1)S(1)}, bf16[16,27,1,256]{3,0,2,1:T(8,128)(2,1)}, u32[]{:S(2)}) %copy-start.2) | copy-done | bytes 221208
  4.7 19.7 %shard_map.67 = (bf16[28,64,256]{2,1,0:T(8,128)(2,1)S(1)}, bf16[28,64,256]{2,1,0:T(8,128)(2,1)S(1)}, bf16[19,64,256]{2,1,0:T(8,128)(2,1)S(1)}, bf16[19,64,256]{2,1,0:T(8,128)(2,1)S(1)}) custom-call(bf16[27,64,256]{2,1,0:T(8,128)(2,1)S(1)} %reshape.130.x_ref, bf16[27,16,256]{2,1,0:T(8,128)(2,1)S(1)} %bitcast.18), custom_call_target="tpu_custom_call" | custom-call | tf_op jit(solution)/shard_map/pallas_call | solution.py:126
  24.4 0.0 copy-start
  24.4 0.8 copy-done
  25.2 0.0 copy-start.1
  25.2 0.1 constant_dynamic-slice_fusion.1
  25.3 0.1 fusion.2
  25.4 0.9 %broadcast_in_dim.34 = f32[16,4,16,4]{3,2,1,0:T(8,128)} broadcast(f32[16,16]{1,0:T(8,128)S(1)} %convert_element_type.7), dimensions={0,2} | broadcast | bytes 17408 | tf_op jit(solution)/shard_map/broadcast_in_dim | solution.py:447
  26.3 0.0 copy-start.3
  26.3 1.3 %reshape.132.mask = f32[64,64]{1,0:T(8,128)S(1)} reshape(f32[16,4,16,4]{3,2,1,0:T(8,128)} %broadcast_in_dim.34) | data formatting | bytes 32768 | tf_op jit(solution)/shard_map/reshape | solution.py:447
  27.6 0.0 copy-done.1
  27.6 0.0 copy-done.3
  27.6 55.9 %shard_map.68 = f32[3,64,64]{2,1,0:T(8,128)S(1)} custom-call(s32[5760]{0:T(1024)S(1)} %reshape.129.table, bf16[28,64,256]{2,1,0:T(8,128)(2,1)S(1)} %get-tuple-element.7.phi, bf16[28,64,256]{2,1,0:T(8,128)(2,1)S(1)} %get-tuple-element.8.hphi, bf16[19,64,256]{2,1,0:T(8,128)(2,1)S(1)} %get-tuple-element.9.bl, bf16[19,64,256]{2,1,0:T(8,128)(2,1)S(1)} %copy-done.1, ...), custom_call_target="tpu_custom_call" | custom-call | tf_op jit(solution)/shard_map/pallas_call | solution.py:389
  83.5 0.6 slice_bitcast_fusion
  (10 shorter events, 0.1 us)
Async XLA Ops:
  0.6 0.7 copy-start.4
  3.8 0.9 %copy-start.2 = (bf16[16,27,1,256]{3,0,2,1:T(8,128)(2,1)S(1)}, bf16[16,27,1,256]{3,0,2,1:T(8,128)(2,1)}, u32[]{:S(2)}) copy-start(bf16[16,27,1,256]{3,0,2,1:T(8,128)(2,1)} %param.5) | copy-start | bytes 663556
  24.4 0.8 copy-start
  25.2 2.3 %copy-start.1 = (bf16[19,64,256]{2,1,0:T(8,128)(2,1)S(1)}, bf16[19,64,256]{2,1,0:T(8,128)(2,1)}, u32[]{:S(2)}) copy-start(bf16[19,64,256]{2,1,0:T(8,128)(2,1)} %copy-done) | copy-start | bytes 1867780
  26.3 1.3 %copy-start.3 = (f32[64,64]{1,0:T(8,128)S(1)}, f32[64,64]{1,0:T(8,128)}, u32[]{:S(2)}) copy-start(f32[64,64]{1,0:T(8,128)} %k0.1) | copy-start | bytes 49156

commit v2 on v1

--- a/solution.py
+++ b/solution.py
@@ -11,6 +11,7 @@
 F32 = jnp.float32
 BF16 = jnp.bfloat16
 GRID_BLOCKS = 180
+BATCH = 12
 ATOMS = 16
 FUNCS = 4
 ROWS = ATOMS * FUNCS
@@ -61,10 +62,19 @@
     )
 
 
-def exchange_kernel(n, x_ref, v_ref, phi, hphi, bl, bu, lo, hi, base, send, recv):
+def interleave(phi, hphi):
+    head = lax.broadcasted_iota(jnp.int32, phi.shape, 0) % 8 < 4
+    even = jnp.where(head, phi, pltpu.roll(hphi, 4, 0))
+    odd = jnp.where(head, pltpu.roll(phi, ROWS - 4, 0), hphi)
+    return jnp.concatenate([even, odd], axis=0).astype(BF16)
+
+
+def exchange_kernel(n, x_ref, v_hbm, both, bl, bu, v_ref, lo, hi, base, v_sem, send, recv):
     s = lax.axis_index("atoms")
     c = lax.axis_index("cols")
     up = lambda at, k: lax.rem(at + k + n, n)
+    load = pltpu.make_async_copy(v_hbm, v_ref, v_sem)
+    load.start()
     for d in (1, -1):
         signal_barrier(s, up(c, d))
         signal_barrier(up(s, d), c)
@@ -78,11 +88,9 @@
     for copy in copies:
         copy.start()
     empty = jnp.zeros((ROWS, 256), BF16)
-    phi[27] = empty
-    hphi[27] = empty
+    both[27] = jnp.concatenate([empty, empty], axis=0)
     bl[18] = empty
     bu[18] = empty
-    phi[0:27] = x_ref[...]
     own, z_low, z_high, y_low, y_high = shift_matrices()
     for bx in range(3):
         first = 9 * bx
@@ -98,6 +106,7 @@
         lax.broadcasted_iota(jnp.int32, (ROWS, ATOMS), 0) // FUNCS
         == lax.broadcasted_iota(jnp.int32, (ROWS, ATOMS), 1)
     ).astype(F32).astype(BF16)
+    load.wait()
     for p in range(27):
         base[p] = -0.5 * base[p] + mm(pick, v_ref[p]) * x_ref[p].astype(F32)
     copies[2].wait_recv()
@@ -113,7 +122,7 @@
             high = hi[p].astype(F32) * (1 - last).astype(F32)
         else:
             high = hi[p + 9 * last].astype(F32)
-        hphi[p] = (base[p] - 0.5 * (low + high)).astype(BF16)
+        both[p] = interleave(x_ref[p].astype(F32), base[p] - 0.5 * (low + high))
     copies[0].wait_recv()
     copies[1].wait_recv()
     for copy in copies:
@@ -122,21 +131,23 @@
 
 def exchange(n, x, v):
     vmem = pl.BlockSpec(memory_space=pltpu.VMEM)
-    blocks = lambda count: jax.ShapeDtypeStruct((count, ROWS, 256), BF16)
+    blocks = lambda count, rows=ROWS: jax.ShapeDtypeStruct((count, rows, 256), BF16)
     return pl.pallas_call(
         functools.partial(exchange_kernel, n),
-        out_shape=(blocks(28), blocks(28), blocks(19), blocks(19)),
-        in_specs=[vmem] * 2,
-        out_specs=(vmem,) * 4,
+        out_shape=(blocks(28, 2 * ROWS), blocks(19), blocks(19)),
+        in_specs=[vmem, pl.BlockSpec(memory_space=pl.ANY)],
+        out_specs=(vmem,) * 3,
         scratch_shapes=[
+            pltpu.VMEM((27, ATOMS, 256), BF16),
             pltpu.VMEM((27, ROWS, 256), BF16),
             pltpu.VMEM((27, ROWS, 256), BF16),
             pltpu.VMEM((27, ROWS, 256), F32),
+            pltpu.SemaphoreType.DMA,
             pltpu.SemaphoreType.DMA((4,)),
             pltpu.SemaphoreType.DMA((4,)),
         ],
         compiler_params=pltpu.CompilerParams(
-            collective_id=1, has_side_effects=True, vmem_limit_bytes=32 * 1024 * 1024
+            collective_id=1, has_side_effects=True, vmem_limit_bytes=16 * 1024 * 1024
         ),
     )(x, v)
 
@@ -164,13 +175,26 @@
     return jnp.concatenate([unpack(ref[t]) for t in range(n)], axis=0)
 
 
-def gram_pass(table, phi, hphi, band, row, start, count, batch):
-    def gather(ref, at, shift):
+def gram_pass(table, both, band, row, start, count):
+    def own(at, k):
+        tiles = []
+        for i in range(8):
+            first, second = (4 * i, 4 * i + 2) if i < 4 else (4 * i - 15, 4 * i - 13)
+            rows = slice(16 * i, 16 * i + 16)
+            tiles.append(
+                jnp.where(
+                    row < 8,
+                    both[table[at, 32 * k + first], rows, :],
+                    both[table[at, 32 * k + second], rows, :],
+                )
+            )
+        return tiles
+
+    def near(at, k):
         tiles = []
         for i in range(4):
-            picked = [
-                ref[table[at + shift + 4 * i + j], 16 * i : 16 * i + 16, :] for j in range(4)
-            ]
+            rows = slice(16 * i, 16 * i + 16)
+            picked = [band[table[at, 32 * k + 16 + 4 * i + j], rows, :] for j in range(4)]
             tiles.append(
                 jnp.where(
                     row < 8,
@@ -178,29 +202,27 @@
                     jnp.where(row < 12, picked[2], picked[3]),
                 )
             )
-        return jnp.concatenate(tiles, axis=0)
-
-    columns = ROWS if band is None else 2 * ROWS
+        return tiles
+
+    columns = 2 * ROWS if band is None else 3 * ROWS
 
     def step(i, acc):
         left, right = [], []
-        for k in range(batch):
-            at = (start + batch * i + k) * 32
-            values = gather(phi, at, 0)
-            left.append(jnp.concatenate([gather(hphi, at, 0), values], axis=0))
-            if band is None:
-                right.append(values)
-            else:
-                right.append(jnp.concatenate([values, gather(band, at, 16)], axis=0))
+        for k in range(BATCH):
+            tiles = own(start // BATCH + i, k)
+            left.append(jnp.concatenate(tiles, axis=0))
+            if band is not None:
+                tiles = tiles + near(start // BATCH + i, k)
+            right.append(jnp.concatenate(tiles, axis=0))
         left = jnp.concatenate(left, axis=1)
         right = jnp.concatenate(right, axis=1)
         return acc + lax.dot_general(left, right, (((1,), (1,)), ((), ())), preferred_element_type=F32)
 
-    return lax.fori_loop(0, count // batch, step, jnp.zeros((2 * ROWS, columns), F32))
+    return lax.fori_loop(0, count // BATCH, step, jnp.zeros((2 * ROWS, columns), F32))
 
 
 def purify_kernel(
-    n, table, phi, hphi, bl, bu, k0, mask, out,
+    n, table, both, bl, bu, k0, near, out,
     part, k0p, rs_buf, piece, ag, k0row, k0n, bblk, ball, y1, y1all, k1, k1all, mrow, mall,
     rs_s, rs_r, ag_s, ag_r, kr_s, kr_r, kn_s, kn_r, b_s, b_r, y_s, y_r, k_s, k_r, m_s, m_r,
 ):
@@ -215,8 +237,18 @@
         signal_barrier(up(s, k), c)
     pairs = [(d, f) for d in range(-2, 3) for f in range(3)]
     k0p[...] = pack(k0[...])
+    spread = (
+        lax.broadcasted_iota(jnp.int32, (ROWS, ATOMS), 0) // FUNCS
+        == lax.broadcasted_iota(jnp.int32, (ROWS, ATOMS), 1)
+    ).astype(F32).astype(BF16)
+    mask = lax.dot_general(
+        mm(spread, near[...].astype(BF16)).astype(BF16),
+        spread,
+        (((1,), (1,)), ((), ())),
+        preferred_element_type=F32,
+    )
     row = lax.broadcasted_iota(jnp.int32, (16, 256), 0).astype(F32).astype(BF16)
-    lower = gram_pass(table, phi, hphi, bl, row, 0, 72, 4)
+    lower = gram_pass(table, both, bl, row, 0, 72)
     pl.semaphore_wait(pltpu.get_barrier_semaphore(), 2 * (n - 1))
     kn_copies = []
     for i, d in enumerate((1, -1)):
@@ -229,14 +261,20 @@
         copy.start()
         kr_copies.append(copy)
     k0row[c] = k0p[...]
-    middle = gram_pass(table, phi, hphi, None, row, 72, 36, 4)
-    upper = gram_pass(table, phi, hphi, bu, row, 108, 72, 4)
-    sums = jnp.concatenate(
-        [lower[:, ROWS:], lower[:, :ROWS] + middle + upper[:, :ROWS], upper[:, ROWS:]], axis=1
+    middle = gram_pass(table, both, None, row, 72, 36)
+    upper = gram_pass(table, both, bu, row, 108, 72)
+    mine = lower[:, : 2 * ROWS] + middle + upper[:, : 2 * ROWS]
+    source = lax.broadcasted_iota(jnp.int32, (2 * ROWS, ROWS), 0)
+    target = lax.broadcasted_iota(jnp.int32, (2 * ROWS, ROWS), 1)
+    atom = target // 4
+    place = 8 * (atom // 2 + 8 * (atom % 2)) + target % 4
+    mine = jnp.dot(
+        mine, (source == place).astype(F32), precision=lax.Precision.HIGHEST, preferred_element_type=F32
     )
+    sums = jnp.concatenate([lower[:, 2 * ROWS :], mine, upper[:, 2 * ROWS :]], axis=1)
     for a in range(ATOMS):
-        part[a, 0:4, :] = sums[ROWS + 4 * a : ROWS + 4 * a + 4, :]
-        part[a, 4:8, :] = sums[4 * a : 4 * a + 4, :]
+        at = 8 * (a // 2 + 8 * (a % 2))
+        part[a] = sums[at : at + 8, :]
 
     rs_copies = []
     for k in range(1, n):
@@ -270,17 +308,6 @@
         copy.start()
         b_copies.append(copy)
     ball[s] = bblk[...]
-    m_sends = []
-    for i, d in enumerate((-2, -1, 1, 2)):
-        target = up(s, d)
-        wanted = up(c - target, 1) < 3
-        copy = remote(mrow, mall.at[2 - d], m_s.at[i], m_r.at[i], target, c)
-        m_sends.append((wanted, copy))
-
-        @pl.when(wanted)
-        def _():
-            copy.start()
-
     inside = jnp.where(active, 1.0, 0.0).astype(F32)
 
     def block(matrix):
@@ -310,6 +337,17 @@
         def _():
             copy.start()
 
+    m_sends = []
+    for i, d in enumerate((-2, -1, 1, 2)):
+        target = up(s, d)
+        wanted = up(c - target, 1) < 3
+        copy = remote(mrow, mall.at[2 - d], m_s.at[i], m_r.at[i], target, c)
+        m_sends.append((wanted, copy))
+
+        @pl.when(wanted)
+        def _():
+            copy.start()
+
     out[2] = jnp.zeros((ROWS, ROWS), F32)
 
     @pl.when(active)
@@ -319,7 +357,7 @@
             other = up(c, k)
             remote(y1, y1all.at[other], y_s.at[0], y_r.at[other], s, other).wait_recv()
         ycat = split(side_by_side(y1all, n))
-        first = mask[...] * (3.0 * y_own - 2.0 * dot3(ycat, bcol))
+        first = mask * (3.0 * y_own - 2.0 * dot3(ycat, bcol))
         k1[...] = pack(first)
         for i, (d, f) in enumerate(pairs):
             t, v = up(s, d), up(s, d + f - 1)
@@ -365,7 +403,7 @@
         y2s = jnp.where(
             e == 0, y2[:, 2 * ROWS : 3 * ROWS], jnp.where(e == 1, y2[:, 3 * ROWS : 4 * ROWS], y2[:, 4 * ROWS : 5 * ROWS])
         )
-        out[2] = mask[...] * (3.0 * y2s - 2.0 * dot3(split(w2), split(kcol)))
+        out[2] = mask * (3.0 * y2s - 2.0 * dot3(split(w2), split(kcol)))
         for i, (d, f) in enumerate(pairs):
             t, v = up(s, d), up(s, d + f - 1)
 
@@ -382,14 +420,14 @@
             copy.wait_send()
 
 
-def purify(n, table, phi, hphi, bl, bu, kernel, mask):
+def purify(n, table, both, bl, bu, kernel, near):
     vmem = pl.BlockSpec(memory_space=pltpu.VMEM)
     dma = pltpu.SemaphoreType.DMA
     half = lambda *lead: pltpu.VMEM((*lead, ROWS // 2, 2 * ROWS), F32)
     return pl.pallas_call(
         functools.partial(purify_kernel, n),
         out_shape=jax.ShapeDtypeStruct((3, ROWS, ROWS), F32),
-        in_specs=[pl.BlockSpec(memory_space=pltpu.SMEM)] + [vmem] * 6,
+        in_specs=[pl.BlockSpec(memory_space=pltpu.SMEM)] + [vmem] * 5,
         out_specs=vmem,
         scratch_shapes=[
             pltpu.VMEM((n, 8, 3 * ROWS), F32),
@@ -412,9 +450,9 @@
             dma((15,)), dma((15,)), dma((4,)), dma((4,)),
         ],
         compiler_params=pltpu.CompilerParams(
-            collective_id=0, has_side_effects=True, vmem_limit_bytes=40 * 1024 * 1024
+            collective_id=0, has_side_effects=True, vmem_limit_bytes=16 * 1024 * 1024
         ),
-    )(table, phi, hphi, bl, bu, kernel, mask)
+    )(table, both, bl, bu, kernel, near)
 
 
 def block_table(band, slab):
@@ -427,7 +465,7 @@
     lower = jnp.where(inside, index - 9, 18)[:, :ATOMS]
     upper = jnp.where(inside, index, 18)[:, 2 * ATOMS :]
     other = jnp.where(blocks[:, None] < 72, lower, upper)
-    return jnp.concatenate([own, other], axis=1).reshape(-1)
+    return jnp.concatenate([own, other], axis=1).reshape(GRID_BLOCKS // BATCH, 32 * BATCH)
 
 
 def local(supports, potential, anchors, kernel):
@@ -436,7 +474,7 @@
     slabs = lax.axis_size("atoms")
     x = supports.transpose(2, 3, 0, 1, 4).reshape(27, ROWS, 256)
     v = potential.transpose(1, 2, 0, 3).reshape(27, ATOMS, 256)
-    phi, hphi, bl, bu = exchange(slabs, x, v)
+    both, bl, bu = exchange(slabs, x, v)
     far = jnp.full((ATOMS, 3), -100, jnp.int32)
     padded = jnp.concatenate([far, anchors, -2 * far], axis=0)
     band = lax.dynamic_slice_in_dim(padded, slab * ATOMS, 3 * ATOMS, 0)
@@ -444,8 +482,7 @@
     rows = lax.dynamic_slice_in_dim(anchors, slab * ATOMS, ATOMS, 0)
     columns = lax.dynamic_slice_in_dim(anchors, col * ATOMS, ATOMS, 0)
     near = jnp.all(jnp.abs(columns[None] - rows[:, None]) <= 2, axis=-1).astype(F32)
-    mask = jnp.broadcast_to(near[:, None, :, None], (ATOMS, FUNCS, ATOMS, FUNCS)).reshape(ROWS, ROWS)
-    out = purify(slabs, table, phi, hphi, bl, bu, kernel, mask)
+    out = purify(slabs, table, both, bl, bu, kernel, near)
     return out[0], out[1], out[2]
 
 

time: 84.3 us -> 79.1 us (0.938)
  Pallas kernels: 75.6 us -> 71.3 us
  local copies, waits for them, and re-layouts: 7.31 us -> 5.64 us
    pallas_call x1, Pallas kernels: 55.9 us -> 50.8 us  [purify(): pl.pallas_call(functools.partial(purify_kernel, n), out_shape=jax.ShapeDt...]
    reshape x2 -> x1, local copies, waits for them, and re-layouts: 1.36 us -> 0.09 us  [block_table(): jnp.concatenate([own, other], axis=1)]
    broadcast_in_dim x1 -> x0, local copies, waits for them, and re-layouts: 0.88 us -> none  [local(): jnp.broadcast_to(near[:, None, :, None], (ATOMS, FUNCS, ATOMS, FUNCS))]
where the time goes in v2:
time: 79.1 us; the launch traced here: 78.8 us
  Pallas kernels  71.3 us (90%)
  local copies, waits for them, and re-layouts  5.64 us (7%)
  other arithmetic  1.11 us (1%)
  between operations  0.81 us (1%)
    pallas_call x1, Pallas kernels, purify(): pl.pallas_call(functools.partial(purify_kernel, n), out_shape=jax.ShapeDt...  50.8 us
    pallas_call x1, Pallas kernels, exchange(): pl.pallas_call(functools.partial(exchange_kernel, n), out_shape=(blocks(2...  20.4 us
    unnamed x10, local copies, waits for them, and re-layouts  2.83 us
    transpose x1, local copies, waits for them, and re-layouts, local(): x = supports.transpose(2, 3, 0, 1, 4).reshape(27, ROWS, 256)  1.62 us

profile of v2, /device:TPU:1, one launch (start us, length us, event | category | flops | bytes accessed | tf_op | source)
XLA Modules:
  0.0 78.8 jit_solution(11489489016447811366)
XLA Ops:
  0.7 0.1 pad_dynamic-slice_fusion.1
  0.7 0.8 fusion.6
  1.6 0.1 broadcast_subtract_fusion
  1.7 0.1 and_reduce_fusion
  1.8 0.1 copy.20
  1.9 0.1 reshape.123.table
  2.0 1.6 %copy.21 = bf16[27,1,16,4,256]{4,3,2,0,1:T(4,128)(2,1)S(1)} copy(bf16[27,1,16,4,256]{4,3,1,0,2:T(4,128)(2,1)} %bitcast.17) | data formatting | bytes 1769472 | tf_op jit(solution)/shard_map/transpose | solution.py:475
  3.7 0.0 copy-start.4
  3.7 0.0 copy-start.3
  3.7 0.2 reshape.124.x_ref
  3.9 0.0 copy-start.2
  3.9 0.9 %copy-done.2 = bf16[16,27,1,256]{3,0,2,1:T(8,128)(2,1)S(1)} copy-done((bf16[16,27,1,256]{3,0,2,1:T(8,128)(2,1)S(1)}, bf16[16,27,1,256]{3,0,2,1:T(8,128)(2,1)}, u32[]{:S(2)}) %copy-start.2) | copy-done | bytes 221208
  4.8 20.4 %shard_map.67 = (bf16[28,128,256]{2,1,0:T(8,128)(2,1)S(1)}, bf16[19,64,256]{2,1,0:T(8,128)(2,1)S(1)}, bf16[19,64,256]{2,1,0:T(8,128)(2,1)S(1)}) custom-call(bf16[27,64,256]{2,1,0:T(8,128)(2,1)S(1)} %reshape.124.x_ref, bf16[27,16,256]{2,1,0:T(8,128)(2,1)S(1)} %bitcast.16), custom_call_target="tpu_custom_call" | custom-call | tf_op jit(solution)/shard_map/pallas_call | solution.py:135
  25.3 0.0 copy-start
  25.3 0.8 %copy-done = bf16[19,64,256]{2,1,0:T(8,128)(2,1)} copy-done((bf16[19,64,256]{2,1,0:T(8,128)(2,1)}, bf16[19,64,256]{2,1,0:T(8,128)(2,1)S(1)}, u32[]{:S(2)}) %copy-start) | copy-done | bytes 622616
  26.1 0.0 copy-done.4
  26.1 0.1 constant_dynamic-slice_fusion.1
  26.2 0.1 fusion.2
  26.3 0.0 copy-done.3
  26.3 0.0 copy-start.1
  26.3 1.1 %copy-done.1 = bf16[19,64,256]{2,1,0:T(8,128)(2,1)S(1)} copy-done((bf16[19,64,256]{2,1,0:T(8,128)(2,1)S(1)}, bf16[19,64,256]{2,1,0:T(8,128)(2,1)}, u32[]{:S(2)}) %copy-start.1) | copy-done | bytes 622616
  27.3 50.8 %shard_map.68 = f32[3,64,64]{2,1,0:T(8,128)S(1)} custom-call(s32[15,384]{1,0:T(8,128)S(1)} %reshape.123.table, bf16[28,128,256]{2,1,0:T(8,128)(2,1)S(1)} %get-tuple-element.6.both, bf16[19,64,256]{2,1,0:T(8,128)(2,1)S(1)} %get-tuple-element.7.bl, bf16[19,64,256]{2,1,0:T(8,128)(2,1)S(1)} %copy-done.1, f32[64,64]{1,0:T(8,128)S(1)} %copy-done.3, ...), custom_call_target="tpu_custom_call" | custom-call | tf_op jit(solution)/shard_map/pallas_call | solution.py:427
  78.2 0.6 slice_bitcast_fusion
  (10 shorter events, 0.1 us)
Async XLA Ops:
  3.7 22.4 %copy-start.4 = (s32[256,3]{0,1:T(4,128)S(1)}, s32[256,3]{0,1:T(4,128)}, u32[]{:S(2)}) copy-start(s32[256,3]{0,1:T(4,128)} %param.6) | copy-start | bytes 9220
  3.7 22.6 %copy-start.3 = (f32[64,64]{1,0:T(8,128)S(1)}, f32[64,64]{1,0:T(8,128)}, u32[]{:S(2)}) copy-start(f32[64,64]{1,0:T(8,128)} %k0.1) | copy-start | bytes 49156
  3.9 0.9 %copy-start.2 = (bf16[16,27,1,256]{3,0,2,1:T(8,128)(2,1)S(1)}, bf16[16,27,1,256]{3,0,2,1:T(8,128)(2,1)}, u32[]{:S(2)}) copy-start(bf16[16,27,1,256]{3,0,2,1:T(8,128)(2,1)} %param.5) | copy-start | bytes 663556
  25.3 0.8 %copy-start = (bf16[19,64,256]{2,1,0:T(8,128)(2,1)}, bf16[19,64,256]{2,1,0:T(8,128)(2,1)S(1)}, u32[]{:S(2)}) copy-start(bf16[19,64,256]{2,1,0:T(8,128)(2,1)S(1)} %get-tuple-element.8.bu) | copy-start | bytes 1867780
  26.3 1.1 %copy-start.1 = (bf16[19,64,256]{2,1,0:T(8,128)(2,1)S(1)}, bf16[19,64,256]{2,1,0:T(8,128)(2,1)}, u32[]{:S(2)}) copy-start(bf16[19,64,256]{2,1,0:T(8,128)(2,1)} %copy-done) | copy-start | bytes 1867780

commit v3 on v2

--- a/solution.py
+++ b/solution.py
@@ -10,8 +10,6 @@
 MESH = pl.DeviceIdType.MESH
 F32 = jnp.float32
 BF16 = jnp.bfloat16
-GRID_BLOCKS = 180
-BATCH = 12
 ATOMS = 16
 FUNCS = 4
 ROWS = ATOMS * FUNCS
@@ -69,28 +67,133 @@
     return jnp.concatenate([even, odd], axis=0).astype(BF16)
 
 
-def exchange_kernel(n, x_ref, v_hbm, both, bl, bu, v_ref, lo, hi, base, v_sem, send, recv):
+def pack(block):
+    return jnp.concatenate([block[: ROWS // 2], block[ROWS // 2 :]], axis=1)
+
+
+def unpack(packed):
+    return jnp.concatenate([packed[:, :ROWS], packed[:, ROWS:]], axis=0)
+
+
+def side_by_side(ref, n):
+    lane = lax.broadcasted_iota(jnp.int32, (ROWS // 2, 2 * ROWS), 1) < ROWS
+    tiles = []
+    for t in range(0, n, 2):
+        even, odd = ref[t], ref[t + 1]
+        top = jnp.where(lane, even, pltpu.roll(odd, ROWS, 1))
+        low = jnp.where(lane, pltpu.roll(even, ROWS, 1), odd)
+        tiles.append(jnp.concatenate([top, low], axis=0))
+    return jnp.concatenate(tiles, axis=1)
+
+
+def stacked(ref, n):
+    return jnp.concatenate([unpack(ref[t]) for t in range(n)], axis=0)
+
+
+def gram_pass(table, both, band, row, start, count):
+    def own(at, k):
+        runs = [both.at[pl.ds(table[at, 32 * k + a], 6)] for a in range(ATOMS)]
+
+        def tiles(z):
+            out = []
+            for i in range(8):
+                first, second = (4 * i, 4 * i + 2) if i < 4 else (4 * i - 15, 4 * i - 13)
+                rows = slice(16 * i, 16 * i + 16)
+                out.append(jnp.where(row < 8, runs[first][z, rows, :], runs[second][z, rows, :]))
+            return out
+
+        return tiles
+
+    def near(at, k):
+        runs = [band.at[pl.ds(table[at, 32 * k + 16 + a], 6)] for a in range(ATOMS)]
+
+        def tiles(z):
+            out = []
+            for i in range(4):
+                rows = slice(16 * i, 16 * i + 16)
+                picked = [runs[4 * i + j][z, rows, :] for j in range(4)]
+                out.append(
+                    jnp.where(
+                        row < 8,
+                        jnp.where(row < 4, picked[0], picked[1]),
+                        jnp.where(row < 12, picked[2], picked[3]),
+                    )
+                )
+            return out
+
+        return tiles
+
+    columns = 2 * ROWS if band is None else 3 * ROWS
+
+    def step(i, acc):
+        left, right = [], []
+        for k in range(2):
+            mine = own(start + i, k)
+            others = None if band is None else near(start + i, k)
+            for z in range(6):
+                tiles = mine(z)
+                left.append(jnp.concatenate(tiles, axis=0))
+                if others is not None:
+                    tiles = tiles + others(z)
+                right.append(jnp.concatenate(tiles, axis=0))
+        left = jnp.concatenate(left, axis=1)
+        right = jnp.concatenate(right, axis=1)
+        return acc + lax.dot_general(left, right, (((1,), (1,)), ((), ())), preferred_element_type=F32)
+
+    return lax.fori_loop(0, count, step, jnp.zeros((2 * ROWS, columns), F32))
+
+
+def slab_kernel(
+    n, table, x_ref, v_hbm, k0, near, out,
+    both, bl, bu, lo, hi, base, v_ref,
+    part, k0p, rs_buf, piece, ag, k0row, k0n, bblk, ball, y1, y1all, k1, k1all, mrow, mall,
+    v_sem, band_s, band_r, halo_s, halo_r, known,
+    rs_s, rs_r, ag_s, ag_r, kr_s, kr_r, kn_s, kn_r, b_s, b_r, y_s, y_r, k_s, k_r, m_s, m_r,
+):
     s = lax.axis_index("atoms")
     c = lax.axis_index("cols")
-    up = lambda at, k: lax.rem(at + k + n, n)
+    up = lambda at, k: lax.rem(at + k + 2 * n, n)
+    e = up(c - s, 1)
+    active = e < 3
+    pairs = [(d, f) for d in range(-2, 3) for f in range(3)]
     load = pltpu.make_async_copy(v_hbm, v_ref, v_sem)
     load.start()
     for d in (1, -1):
         signal_barrier(s, up(c, d))
         signal_barrier(up(s, d), c)
+    k0p[...] = pack(k0[...])
     pl.semaphore_wait(pltpu.get_barrier_semaphore(), 4)
-    copies = [
-        remote(x_ref.at[9:27], bl.at[0:18], send.at[0], recv.at[0], up(s, 1), c),
-        remote(x_ref.at[0:18], bu.at[0:18], send.at[1], recv.at[1], up(s, -1), c),
-        remote(x_ref, lo, send.at[2], recv.at[2], s, up(c, 1)),
-        remote(x_ref, hi, send.at[3], recv.at[3], s, up(c, -1)),
+
+    halo = [
+        remote(x_ref, lo, halo_s.at[0], halo_r.at[0], s, up(c, 1)),
+        remote(x_ref, hi, halo_s.at[1], halo_r.at[1], s, up(c, -1)),
     ]
-    for copy in copies:
-        copy.start()
-    empty = jnp.zeros((ROWS, 256), BF16)
-    both[27] = jnp.concatenate([empty, empty], axis=0)
-    bl[18] = empty
-    bu[18] = empty
+    for copy in halo:
+        copy.start()
+    band_copies = []
+    for k in range(6):
+        source, target = x_ref.at[9 + 3 * k : 12 + 3 * k], bl.at[9 * k + 3 : 9 * k + 6]
+        band_copies.append(remote(source, target, band_s.at[k], band_r.at[k], up(s, 1), c))
+        source, target = x_ref.at[3 * k : 3 * k + 3], bu.at[9 * k + 3 : 9 * k + 6]
+        band_copies.append(remote(source, target, band_s.at[6 + k], band_r.at[6 + k], up(s, -1), c))
+    for copy in band_copies:
+        copy.start()
+    kn_copies = []
+    for i, d in enumerate((1, -1)):
+        copy = remote(k0p, k0n.at[i], kn_s.at[i], kn_r.at[i], up(s, d), c)
+        copy.start()
+        kn_copies.append(copy)
+
+    def tell(step):
+        for d in (1 << step, -(1 << step)):
+            pl.semaphore_signal(known.at[step], inc=1, device_id=(s, up(c, d)), device_id_type=MESH)
+            pl.semaphore_signal(known.at[3 + step], inc=1, device_id=(up(s, d), c), device_id_type=MESH)
+
+    def learn(step):
+        pl.semaphore_wait(known.at[step], 2)
+        pl.semaphore_wait(known.at[3 + step], 2)
+
+    tell(0)
     own, z_low, z_high, y_low, y_high = shift_matrices()
     for bx in range(3):
         first = 9 * bx
@@ -102,15 +205,41 @@
             base[first + f : first + f + 2] += mm(rows(f + 1, 2), z_high).reshape(2, ROWS, 256)
         base[first + 3 : first + 9] += mm(rows(0, 6), y_low).reshape(6, ROWS, 256)
         base[first : first + 6] += mm(rows(3, 6), y_high).reshape(6, ROWS, 256)
-    pick = (
+    learn(0)
+    tell(1)
+    spread = (
         lax.broadcasted_iota(jnp.int32, (ROWS, ATOMS), 0) // FUNCS
         == lax.broadcasted_iota(jnp.int32, (ROWS, ATOMS), 1)
     ).astype(F32).astype(BF16)
     load.wait()
     for p in range(27):
-        base[p] = -0.5 * base[p] + mm(pick, v_ref[p]) * x_ref[p].astype(F32)
-    copies[2].wait_recv()
-    copies[3].wait_recv()
+        base[p] = -0.5 * base[p] + mm(spread, v_ref[p]) * x_ref[p].astype(F32)
+    learn(1)
+    tell(2)
+    for at in range(0, 81, 9):
+        both[at : at + 3] = jnp.zeros((3, 2 * ROWS, 256), BF16)
+        both[at + 6 : at + 9] = jnp.zeros((3, 2 * ROWS, 256), BF16)
+    both[81:90] = jnp.zeros((9, 2 * ROWS, 256), BF16)
+    for ref in (bl, bu):
+        for at in range(0, 54, 9):
+            ref[at : at + 3] = jnp.zeros((3, ROWS, 256), BF16)
+            ref[at + 6 : at + 9] = jnp.zeros((3, ROWS, 256), BF16)
+        ref[54:63] = jnp.zeros((9, ROWS, 256), BF16)
+    mask = lax.dot_general(
+        mm(spread, near[...].astype(BF16)).astype(BF16),
+        spread,
+        (((1,), (1,)), ((), ())),
+        preferred_element_type=F32,
+    )
+    learn(2)
+    kr_copies = []
+    for k in range(1, n):
+        copy = remote(k0p, k0row.at[c], kr_s.at[k - 1], kr_r.at[k - 1], s, up(c, k))
+        copy.start()
+        kr_copies.append(copy)
+    k0row[c] = k0p[...]
+    for copy in halo:
+        copy.wait_recv()
     first = jnp.where(c == 0, 1, 0)
     last = jnp.where(c == n - 1, 1, 0)
     for p in range(27):
@@ -122,147 +251,13 @@
             high = hi[p].astype(F32) * (1 - last).astype(F32)
         else:
             high = hi[p + 9 * last].astype(F32)
-        both[p] = interleave(x_ref[p].astype(F32), base[p] - 0.5 * (low + high))
-    copies[0].wait_recv()
-    copies[1].wait_recv()
-    for copy in copies:
-        copy.wait_send()
-
-
-def exchange(n, x, v):
-    vmem = pl.BlockSpec(memory_space=pltpu.VMEM)
-    blocks = lambda count, rows=ROWS: jax.ShapeDtypeStruct((count, rows, 256), BF16)
-    return pl.pallas_call(
-        functools.partial(exchange_kernel, n),
-        out_shape=(blocks(28, 2 * ROWS), blocks(19), blocks(19)),
-        in_specs=[vmem, pl.BlockSpec(memory_space=pl.ANY)],
-        out_specs=(vmem,) * 3,
-        scratch_shapes=[
-            pltpu.VMEM((27, ATOMS, 256), BF16),
-            pltpu.VMEM((27, ROWS, 256), BF16),
-            pltpu.VMEM((27, ROWS, 256), BF16),
-            pltpu.VMEM((27, ROWS, 256), F32),
-            pltpu.SemaphoreType.DMA,
-            pltpu.SemaphoreType.DMA((4,)),
-            pltpu.SemaphoreType.DMA((4,)),
-        ],
-        compiler_params=pltpu.CompilerParams(
-            collective_id=1, has_side_effects=True, vmem_limit_bytes=16 * 1024 * 1024
-        ),
-    )(x, v)
-
-
-def pack(block):
-    return jnp.concatenate([block[: ROWS // 2], block[ROWS // 2 :]], axis=1)
-
-
-def unpack(packed):
-    return jnp.concatenate([packed[:, :ROWS], packed[:, ROWS:]], axis=0)
-
-
-def side_by_side(ref, n):
-    lane = lax.broadcasted_iota(jnp.int32, (ROWS // 2, 2 * ROWS), 1) < ROWS
-    tiles = []
-    for t in range(0, n, 2):
-        even, odd = ref[t], ref[t + 1]
-        top = jnp.where(lane, even, pltpu.roll(odd, ROWS, 1))
-        low = jnp.where(lane, pltpu.roll(even, ROWS, 1), odd)
-        tiles.append(jnp.concatenate([top, low], axis=0))
-    return jnp.concatenate(tiles, axis=1)
-
-
-def stacked(ref, n):
-    return jnp.concatenate([unpack(ref[t]) for t in range(n)], axis=0)
-
-
-def gram_pass(table, both, band, row, start, count):
-    def own(at, k):
-        tiles = []
-        for i in range(8):
-            first, second = (4 * i, 4 * i + 2) if i < 4 else (4 * i - 15, 4 * i - 13)
-            rows = slice(16 * i, 16 * i + 16)
-            tiles.append(
-                jnp.where(
-                    row < 8,
-                    both[table[at, 32 * k + first], rows, :],
-                    both[table[at, 32 * k + second], rows, :],
-                )
-            )
-        return tiles
-
-    def near(at, k):
-        tiles = []
-        for i in range(4):
-            rows = slice(16 * i, 16 * i + 16)
-            picked = [band[table[at, 32 * k + 16 + 4 * i + j], rows, :] for j in range(4)]
-            tiles.append(
-                jnp.where(
-                    row < 8,
-                    jnp.where(row < 4, picked[0], picked[1]),
-                    jnp.where(row < 12, picked[2], picked[3]),
-                )
-            )
-        return tiles
-
-    columns = 2 * ROWS if band is None else 3 * ROWS
-
-    def step(i, acc):
-        left, right = [], []
-        for k in range(BATCH):
-            tiles = own(start // BATCH + i, k)
-            left.append(jnp.concatenate(tiles, axis=0))
-            if band is not None:
-                tiles = tiles + near(start // BATCH + i, k)
-            right.append(jnp.concatenate(tiles, axis=0))
-        left = jnp.concatenate(left, axis=1)
-        right = jnp.concatenate(right, axis=1)
-        return acc + lax.dot_general(left, right, (((1,), (1,)), ((), ())), preferred_element_type=F32)
-
-    return lax.fori_loop(0, count // BATCH, step, jnp.zeros((2 * ROWS, columns), F32))
-
-
-def purify_kernel(
-    n, table, both, bl, bu, k0, near, out,
-    part, k0p, rs_buf, piece, ag, k0row, k0n, bblk, ball, y1, y1all, k1, k1all, mrow, mall,
-    rs_s, rs_r, ag_s, ag_r, kr_s, kr_r, kn_s, kn_r, b_s, b_r, y_s, y_r, k_s, k_r, m_s, m_r,
-):
-    s = lax.axis_index("atoms")
-    c = lax.axis_index("cols")
-    up = lambda base, k: lax.rem(base + k + 2 * n, n)
-    e = up(c - s, 1)
-    active = e < 3
-
-    for k in range(1, n):
-        signal_barrier(s, up(c, k))
-        signal_barrier(up(s, k), c)
-    pairs = [(d, f) for d in range(-2, 3) for f in range(3)]
-    k0p[...] = pack(k0[...])
-    spread = (
-        lax.broadcasted_iota(jnp.int32, (ROWS, ATOMS), 0) // FUNCS
-        == lax.broadcasted_iota(jnp.int32, (ROWS, ATOMS), 1)
-    ).astype(F32).astype(BF16)
-    mask = lax.dot_general(
-        mm(spread, near[...].astype(BF16)).astype(BF16),
-        spread,
-        (((1,), (1,)), ((), ())),
-        preferred_element_type=F32,
-    )
+        both[9 * (p // 3) + 3 + p % 3] = interleave(x_ref[p].astype(F32), base[p] - 0.5 * (low + high))
     row = lax.broadcasted_iota(jnp.int32, (16, 256), 0).astype(F32).astype(BF16)
-    lower = gram_pass(table, both, bl, row, 0, 72)
-    pl.semaphore_wait(pltpu.get_barrier_semaphore(), 2 * (n - 1))
-    kn_copies = []
-    for i, d in enumerate((1, -1)):
-        copy = remote(k0p, k0n.at[i], kn_s.at[i], kn_r.at[i], up(s, d), c)
-        copy.start()
-        kn_copies.append(copy)
-    kr_copies = []
-    for k in range(1, n):
-        copy = remote(k0p, k0row.at[c], kr_s.at[k - 1], kr_r.at[k - 1], s, up(c, k))
-        copy.start()
-        kr_copies.append(copy)
-    k0row[c] = k0p[...]
-    middle = gram_pass(table, both, None, row, 72, 36)
-    upper = gram_pass(table, both, bu, row, 108, 72)
+    middle = gram_pass(table, both, None, row, 6, 3)
+    for copy in band_copies:
+        copy.wait_recv()
+    lower = gram_pass(table, both, bl, row, 0, 6)
+    upper = gram_pass(table, both, bu, row, 9, 6)
     mine = lower[:, : 2 * ROWS] + middle + upper[:, : 2 * ROWS]
     source = lax.broadcasted_iota(jnp.int32, (2 * ROWS, ROWS), 0)
     target = lax.broadcasted_iota(jnp.int32, (2 * ROWS, ROWS), 1)
@@ -411,7 +406,7 @@
             def _():
                 remote(k1, k1all.at[(2 - d) * 3 + e], k_s.at[i], k_r.at[i], t, v).wait_send()
 
-    for copy in rs_copies + kn_copies + kr_copies + ag_copies + b_copies:
+    for copy in halo + band_copies + rs_copies + kn_copies + kr_copies + ag_copies + b_copies:
         copy.wait_send()
     for wanted, copy in m_sends + y_sends:
 
@@ -420,16 +415,30 @@
             copy.wait_send()
 
 
-def purify(n, table, both, bl, bu, kernel, near):
+def slab_program(n, table, x, v, kernel, near):
     vmem = pl.BlockSpec(memory_space=pltpu.VMEM)
     dma = pltpu.SemaphoreType.DMA
+    blocks = lambda count, rows=ROWS, kind=BF16: pltpu.VMEM((count, rows, 256), kind)
     half = lambda *lead: pltpu.VMEM((*lead, ROWS // 2, 2 * ROWS), F32)
     return pl.pallas_call(
-        functools.partial(purify_kernel, n),
+        functools.partial(slab_kernel, n),
         out_shape=jax.ShapeDtypeStruct((3, ROWS, ROWS), F32),
-        in_specs=[pl.BlockSpec(memory_space=pltpu.SMEM)] + [vmem] * 5,
+        in_specs=[
+            pl.BlockSpec(memory_space=pltpu.SMEM),
+            vmem,
+            pl.BlockSpec(memory_space=pl.ANY),
+            vmem,
+            vmem,
+        ],
         out_specs=vmem,
         scratch_shapes=[
+            blocks(90, 2 * ROWS),
+            blocks(63),
+            blocks(63),
+            blocks(27),
+            blocks(27),
+            blocks(27, kind=F32),
+            blocks(27, ATOMS),
             pltpu.VMEM((n, 8, 3 * ROWS), F32),
             half(),
             pltpu.VMEM((n - 1, 8, 3 * ROWS), F32),
@@ -445,44 +454,44 @@
             half(15),
             pltpu.VMEM((ROWS, 3 * ROWS), F32),
             pltpu.VMEM((5, ROWS, 3 * ROWS), F32),
+            dma, dma((12,)), dma((12,)), dma((2,)), dma((2,)),
+            pltpu.SemaphoreType.REGULAR((6,)),
             dma((n,)), dma((n,)), dma((n,)), dma((n,)), dma((n,)), dma((n,)),
             dma((2,)), dma((2,)), dma((n,)), dma((n,)), dma((3,)), dma((n,)),
             dma((15,)), dma((15,)), dma((4,)), dma((4,)),
         ],
         compiler_params=pltpu.CompilerParams(
-            collective_id=0, has_side_effects=True, vmem_limit_bytes=16 * 1024 * 1024
+            collective_id=0, has_side_effects=True, vmem_limit_bytes=40 * 1024 * 1024
         ),
-    )(table, both, bl, bu, kernel, near)
-
-
-def block_table(band, slab):
-    blocks = jnp.arange(GRID_BLOCKS, dtype=jnp.int32)
-    place = jnp.stack([blocks // 36 + 3 * slab, blocks // 6 % 6, blocks % 6], axis=-1)
-    offset = place[:, None, :] - band[None, :, :]
+    )(table, x, v, kernel, near)
+
+
+def run_table(band, slab):
+    cells = jnp.arange(30, dtype=jnp.int32)
+    place = jnp.stack([cells // 6 + 3 * slab, cells % 6], axis=-1)
+    offset = place[:, None, :] - band[None, :, :2]
     inside = jnp.all((offset >= 0) & (offset <= 2), axis=-1)
-    index = offset[..., 0] * 9 + offset[..., 1] * 3 + offset[..., 2]
-    own = jnp.where(inside, index, 27)[:, ATOMS : 2 * ATOMS]
-    lower = jnp.where(inside, index - 9, 18)[:, :ATOMS]
-    upper = jnp.where(inside, index, 18)[:, 2 * ATOMS :]
-    other = jnp.where(blocks[:, None] < 72, lower, upper)
-    return jnp.concatenate([own, other], axis=1).reshape(GRID_BLOCKS // BATCH, 32 * BATCH)
+    start = (offset[..., 0] * 3 + offset[..., 1]) * 9 + 3 - band[None, :, 2]
+    own = jnp.where(inside, start, 81)[:, ATOMS : 2 * ATOMS]
+    lower = jnp.where(inside, start - 27, 54)[:, :ATOMS]
+    upper = jnp.where(inside, start, 54)[:, 2 * ATOMS :]
+    other = jnp.where(cells[:, None] < 12, lower, jnp.where(cells[:, None] < 18, 54, upper))
+    return jnp.concatenate([own, other], axis=1).reshape(15, 64)
 
 
 def local(supports, potential, anchors, kernel):
     slab = lax.axis_index("atoms")
     col = lax.axis_index("cols")
-    slabs = lax.axis_size("atoms")
     x = supports.transpose(2, 3, 0, 1, 4).reshape(27, ROWS, 256)
     v = potential.transpose(1, 2, 0, 3).reshape(27, ATOMS, 256)
-    both, bl, bu = exchange(slabs, x, v)
     far = jnp.full((ATOMS, 3), -100, jnp.int32)
     padded = jnp.concatenate([far, anchors, -2 * far], axis=0)
     band = lax.dynamic_slice_in_dim(padded, slab * ATOMS, 3 * ATOMS, 0)
-    table = block_table(band, slab)
+    table = run_table(band, slab)
     rows = lax.dynamic_slice_in_dim(anchors, slab * ATOMS, ATOMS, 0)
     columns = lax.dynamic_slice_in_dim(anchors, col * ATOMS, ATOMS, 0)
     near = jnp.all(jnp.abs(columns[None] - rows[:, None]) <= 2, axis=-1).astype(F32)
-    out = purify(slabs, table, both, bl, bu, kernel, near)
+    out = slab_program(lax.axis_size("atoms"), table, x, v, kernel, near)
     return out[0], out[1], out[2]
 
 

time: 79.1 us -> 74.5 us (0.942)
  Pallas kernels: 71.3 us -> 69.1 us
  local copies, waits for them, and re-layouts: 5.64 us -> 3.9 us
    pallas_call x2 -> x1, Pallas kernels: 71.3 us -> 69.1 us  [slab_program(): pl.pallas_call(functools.partial(slab_kernel, n), out_shape=jax.ShapeDtyp...]
    unnamed x10 -> x6, local copies, waits for them, and re-layouts: 2.83 us -> 1.18 us
where the time goes in v3:
time: 74.5 us; the launch traced here: 74.3 us
  Pallas kernels  69.1 us (93%)
  local copies, waits for them, and re-layouts  3.9 us (5%)
  between operations  0.76 us (1%)
    pallas_call x1, Pallas kernels, slab_program(): pl.pallas_call(functools.partial(slab_kernel, n), out_shape=jax.ShapeDtyp...  69.1 us
    transpose x1, local copies, waits for them, and re-layouts, local(): x = supports.transpose(2, 3, 0, 1, 4).reshape(27, ROWS, 256)  1.62 us

profile of v3, /device:TPU:1, one launch (start us, length us, event | category | flops | bytes accessed | tf_op | source)
XLA Modules:
  0.0 74.3 jit_solution(9821234895219003582)
XLA Ops:
  0.6 0.0 copy-start.2
  0.7 0.1 pad_dynamic-slice_fusion.1
  0.8 0.6 copy-done.2
  1.3 0.1 fusion.9
  1.4 0.1 broadcast_subtract_fusion
  1.6 0.1 and_reduce_fusion
  1.6 0.1 slice_select_fusion.1
  1.7 0.1 pad_add_fusion
  1.8 0.1 reshape.87.table
  1.9 1.6 %copy.11 = bf16[27,1,16,4,256]{4,3,2,0,1:T(4,128)(2,1)S(1)} copy(bf16[27,1,16,4,256]{4,3,1,0,2:T(4,128)(2,1)} %bitcast.21) | data formatting | bytes 1769472 | tf_op jit(solution)/shard_map/transpose | solution.py:485
  3.5 0.0 copy-start
  3.5 0.2 reshape.88.x_ref
  3.7 0.0 copy-start.1
  3.8 0.1 constant_dynamic-slice_fusion.1
  3.8 0.1 fusion
  3.9 0.5 copy-done
  4.5 0.1 copy-done.1
  4.5 69.1 %shard_map.67 = f32[3,64,64]{2,1,0:T(8,128)S(1)} custom-call(s32[15,64]{1,0:T(8,128)S(1)} %reshape.87.table, bf16[27,64,256]{2,1,0:T(8,128)(2,1)S(1)} %reshape.88.x_ref, bf16[27,16,256]{2,1,0:T(8,128)(2,1)S(1)} %bitcast.20, f32[64,64]{1,0:T(8,128)S(1)} %copy-done.1, f32[16,16]{1,0:T(8,128)S(1)} %convert_element_type.3.near), custom_call_target="tpu_custom_call" | custom-call | tf_op jit(solution)/shard_map/pallas_call | solution.py:423
  73.6 0.6 slice_bitcast_fusion
  (9 shorter events, 0.1 us)
Async XLA Ops:
  0.6 0.7 copy-start.2
  3.5 0.9 %copy-start = (bf16[16,27,1,256]{3,0,2,1:T(8,128)(2,1)S(1)}, bf16[16,27,1,256]{3,0,2,1:T(8,128)(2,1)}, u32[]{:S(2)}) copy-start(bf16[16,27,1,256]{3,0,2,1:T(8,128)(2,1)} %param.5) | copy-start | bytes 663556
  3.7 0.8 %copy-start.1 = (f32[64,64]{1,0:T(8,128)S(1)}, f32[64,64]{1,0:T(8,128)}, u32[]{:S(2)}) copy-start(f32[64,64]{1,0:T(8,128)} %k0.1) | copy-start | bytes 49156

commit v4 on v3

--- a/solution.py
+++ b/solution.py
@@ -60,13 +60,6 @@
     )
 
 
-def interleave(phi, hphi):
-    head = lax.broadcasted_iota(jnp.int32, phi.shape, 0) % 8 < 4
-    even = jnp.where(head, phi, pltpu.roll(hphi, 4, 0))
-    odd = jnp.where(head, pltpu.roll(phi, ROWS - 4, 0), hphi)
-    return jnp.concatenate([even, odd], axis=0).astype(BF16)
-
-
 def pack(block):
     return jnp.concatenate([block[: ROWS // 2], block[ROWS // 2 :]], axis=1)
 
@@ -90,65 +83,75 @@
     return jnp.concatenate([unpack(ref[t]) for t in range(n)], axis=0)
 
 
-def gram_pass(table, both, band, row, start, count):
-    def own(at, k):
-        runs = [both.at[pl.ds(table[at, 32 * k + a], 6)] for a in range(ATOMS)]
-
-        def tiles(z):
-            out = []
-            for i in range(8):
-                first, second = (4 * i, 4 * i + 2) if i < 4 else (4 * i - 15, 4 * i - 13)
-                rows = slice(16 * i, 16 * i + 16)
-                out.append(jnp.where(row < 8, runs[first][z, rows, :], runs[second][z, rows, :]))
-            return out
-
-        return tiles
-
-    def near(at, k):
-        runs = [band.at[pl.ds(table[at, 32 * k + 16 + a], 6)] for a in range(ATOMS)]
-
-        def tiles(z):
-            out = []
-            for i in range(4):
-                rows = slice(16 * i, 16 * i + 16)
-                picked = [runs[4 * i + j][z, rows, :] for j in range(4)]
-                out.append(
-                    jnp.where(
-                        row < 8,
-                        jnp.where(row < 4, picked[0], picked[1]),
-                        jnp.where(row < 12, picked[2], picked[3]),
-                    )
+def gather(table, row, ref, at, shift):
+    runs = [ref.at[pl.ds(table[at, shift + a], 6)] for a in range(ATOMS)]
+
+    def block(z):
+        tiles = []
+        for i in range(4):
+            rows = slice(16 * i, 16 * i + 16)
+            picked = [runs[4 * i + j][z, rows, :] for j in range(4)]
+            tiles.append(
+                jnp.where(
+                    row < 8,
+                    jnp.where(row < 4, picked[0], picked[1]),
+                    jnp.where(row < 12, picked[2], picked[3]),
                 )
-            return out
-
-        return tiles
-
-    columns = 2 * ROWS if band is None else 3 * ROWS
+            )
+        return jnp.concatenate(tiles, axis=0)
+
+    return block
+
+
+def products(table, start, count, left, own, band):
+    row = lax.broadcasted_iota(jnp.int32, (16, 256), 0).astype(F32).astype(BF16)
+    columns = ROWS * ((own is not None) + (band is not None))
 
     def step(i, acc):
-        left, right = [], []
+        lefts, rights = [], []
         for k in range(2):
-            mine = own(start + i, k)
-            others = None if band is None else near(start + i, k)
+            at = start + i
+            left_of = gather(table, row, left, at, 32 * k)
+            own_of = None if own is None or own is left else gather(table, row, own, at, 32 * k)
+            band_of = None if band is None else gather(table, row, band, at, 32 * k + 16)
             for z in range(6):
-                tiles = mine(z)
-                left.append(jnp.concatenate(tiles, axis=0))
-                if others is not None:
-                    tiles = tiles + others(z)
-                right.append(jnp.concatenate(tiles, axis=0))
-        left = jnp.concatenate(left, axis=1)
-        right = jnp.concatenate(right, axis=1)
-        return acc + lax.dot_general(left, right, (((1,), (1,)), ((), ())), preferred_element_type=F32)
-
-    return lax.fori_loop(0, count, step, jnp.zeros((2 * ROWS, columns), F32))
+                first = left_of(z)
+                lefts.append(first)
+                parts = []
+                if own is not None:
+                    parts.append(first if own is left else own_of(z))
+                if band is not None:
+                    parts.append(band_of(z))
+                rights.append(jnp.concatenate(parts, axis=0))
+        return acc + lax.dot_general(
+            jnp.concatenate(lefts, axis=1),
+            jnp.concatenate(rights, axis=1),
+            (((1,), (1,)), ((), ())),
+            preferred_element_type=F32,
+        )
+
+    return lax.fori_loop(0, count, step, jnp.zeros((ROWS, columns), F32))
+
+
+def to_pieces(ref, matrix):
+    for a in range(ATOMS):
+        ref[a, 0:4, :] = matrix[4 * a : 4 * a + 4, : 2 * ROWS]
+        ref[a, 4:8, 0:ROWS] = matrix[4 * a : 4 * a + 4, 2 * ROWS :]
+        ref[a, 4:8, ROWS:] = jnp.zeros((4, ROWS), F32)
+
+
+def from_pieces(ref, rows):
+    for a in range(ATOMS):
+        rows[4 * a : 4 * a + 4, 0 : 2 * ROWS] = ref[a, 0:4, :]
+        rows[4 * a : 4 * a + 4, 2 * ROWS :] = ref[a, 4:8, 0:ROWS]
 
 
 def slab_kernel(
     n, table, x_ref, v_hbm, k0, near, out,
-    both, bl, bu, lo, hi, base, v_ref,
-    part, k0p, rs_buf, piece, ag, k0row, k0n, bblk, ball, y1, y1all, k1, k1all, mrow, mall,
+    phi, hphi, bl, bu, lo, hi, base, v_ref,
+    part, k0p, rs_buf, piece, ag, part_h, rs_buf_h, piece_h, ag_h, hrow, k0row, k0n, bblk, ball, y1, y1all, k1, k1all, mrow, mall,
     v_sem, band_s, band_r, halo_s, halo_r, known,
-    rs_s, rs_r, ag_s, ag_r, kr_s, kr_r, kn_s, kn_r, b_s, b_r, y_s, y_r, k_s, k_r, m_s, m_r,
+    rs_s, rs_r, ag_s, ag_r, rh_s, rh_r, ah_s, ah_r, kr_s, kr_r, kn_s, kn_r, b_s, b_r, y_s, y_r, k_s, k_r, m_s, m_r,
 ):
     s = lax.axis_index("atoms")
     c = lax.axis_index("cols")
@@ -164,6 +167,16 @@
     k0p[...] = pack(k0[...])
     pl.semaphore_wait(pltpu.get_barrier_semaphore(), 4)
 
+    def tell(step):
+        for d in (1 << step, -(1 << step)):
+            pl.semaphore_signal(known.at[step], inc=1, device_id=(s, up(c, d)), device_id_type=MESH)
+            pl.semaphore_signal(known.at[3 + step], inc=1, device_id=(up(s, d), c), device_id_type=MESH)
+
+    def learn(step):
+        pl.semaphore_wait(known.at[step], 2)
+        pl.semaphore_wait(known.at[3 + step], 2)
+
+    tell(0)
     halo = [
         remote(x_ref, lo, halo_s.at[0], halo_r.at[0], s, up(c, 1)),
         remote(x_ref, hi, halo_s.at[1], halo_r.at[1], s, up(c, -1)),
@@ -184,16 +197,8 @@
         copy.start()
         kn_copies.append(copy)
 
-    def tell(step):
-        for d in (1 << step, -(1 << step)):
-            pl.semaphore_signal(known.at[step], inc=1, device_id=(s, up(c, d)), device_id_type=MESH)
-            pl.semaphore_signal(known.at[3 + step], inc=1, device_id=(up(s, d), c), device_id_type=MESH)
-
-    def learn(step):
-        pl.semaphore_wait(known.at[step], 2)
-        pl.semaphore_wait(known.at[3 + step], 2)
-
-    tell(0)
+    learn(0)
+    tell(1)
     own, z_low, z_high, y_low, y_high = shift_matrices()
     for bx in range(3):
         first = 9 * bx
@@ -205,21 +210,30 @@
             base[first + f : first + f + 2] += mm(rows(f + 1, 2), z_high).reshape(2, ROWS, 256)
         base[first + 3 : first + 9] += mm(rows(0, 6), y_low).reshape(6, ROWS, 256)
         base[first : first + 6] += mm(rows(3, 6), y_high).reshape(6, ROWS, 256)
-    learn(0)
-    tell(1)
+        if bx == 0:
+            learn(1)
+            tell(2)
     spread = (
         lax.broadcasted_iota(jnp.int32, (ROWS, ATOMS), 0) // FUNCS
         == lax.broadcasted_iota(jnp.int32, (ROWS, ATOMS), 1)
     ).astype(F32).astype(BF16)
+    learn(2)
+    kr_copies = []
+    for k in range(1, n):
+        copy = remote(k0p, k0row.at[c], kr_s.at[k - 1], kr_r.at[k - 1], s, up(c, k))
+        copy.start()
+        kr_copies.append(copy)
+    k0row[c] = k0p[...]
     load.wait()
     for p in range(27):
         base[p] = -0.5 * base[p] + mm(spread, v_ref[p]) * x_ref[p].astype(F32)
-    learn(1)
-    tell(2)
-    for at in range(0, 81, 9):
-        both[at : at + 3] = jnp.zeros((3, 2 * ROWS, 256), BF16)
-        both[at + 6 : at + 9] = jnp.zeros((3, 2 * ROWS, 256), BF16)
-    both[81:90] = jnp.zeros((9, 2 * ROWS, 256), BF16)
+    for p in range(27):
+        phi[9 * (p // 3) + 3 + p % 3] = x_ref[p]
+    for ref in (phi, hphi):
+        for at in range(0, 81, 9):
+            ref[at : at + 3] = jnp.zeros((3, ROWS, 256), BF16)
+            ref[at + 6 : at + 9] = jnp.zeros((3, ROWS, 256), BF16)
+        ref[81:90] = jnp.zeros((9, ROWS, 256), BF16)
     for ref in (bl, bu):
         for at in range(0, 54, 9):
             ref[at : at + 3] = jnp.zeros((3, ROWS, 256), BF16)
@@ -231,13 +245,19 @@
         (((1,), (1,)), ((), ())),
         preferred_element_type=F32,
     )
-    learn(2)
-    kr_copies = []
-    for k in range(1, n):
-        copy = remote(k0p, k0row.at[c], kr_s.at[k - 1], kr_r.at[k - 1], s, up(c, k))
-        copy.start()
-        kr_copies.append(copy)
-    k0row[c] = k0p[...]
+    s_own = products(table, 0, 15, phi, phi, None)
+    for copy in band_copies:
+        copy.wait_recv()
+    s_low = products(table, 0, 6, phi, None, bl)
+    s_up = products(table, 9, 6, phi, None, bu)
+    to_pieces(part, jnp.concatenate([s_low, s_own, s_up], axis=1))
+
+    rs_copies = []
+    for k in range(1, n):
+        col = up(c, k)
+        copy = remote(part.at[col], rs_buf.at[k - 1], rs_s.at[k - 1], rs_r.at[k - 1], s, col)
+        copy.start()
+        rs_copies.append(copy)
     for copy in halo:
         copy.wait_recv()
     first = jnp.where(c == 0, 1, 0)
@@ -251,32 +271,9 @@
             high = hi[p].astype(F32) * (1 - last).astype(F32)
         else:
             high = hi[p + 9 * last].astype(F32)
-        both[9 * (p // 3) + 3 + p % 3] = interleave(x_ref[p].astype(F32), base[p] - 0.5 * (low + high))
-    row = lax.broadcasted_iota(jnp.int32, (16, 256), 0).astype(F32).astype(BF16)
-    middle = gram_pass(table, both, None, row, 6, 3)
-    for copy in band_copies:
-        copy.wait_recv()
-    lower = gram_pass(table, both, bl, row, 0, 6)
-    upper = gram_pass(table, both, bu, row, 9, 6)
-    mine = lower[:, : 2 * ROWS] + middle + upper[:, : 2 * ROWS]
-    source = lax.broadcasted_iota(jnp.int32, (2 * ROWS, ROWS), 0)
-    target = lax.broadcasted_iota(jnp.int32, (2 * ROWS, ROWS), 1)
-    atom = target // 4
-    place = 8 * (atom // 2 + 8 * (atom % 2)) + target % 4
-    mine = jnp.dot(
-        mine, (source == place).astype(F32), precision=lax.Precision.HIGHEST, preferred_element_type=F32
-    )
-    sums = jnp.concatenate([lower[:, 2 * ROWS :], mine, upper[:, 2 * ROWS :]], axis=1)
-    for a in range(ATOMS):
-        at = 8 * (a // 2 + 8 * (a % 2))
-        part[a] = sums[at : at + 8, :]
-
-    rs_copies = []
-    for k in range(1, n):
-        col = up(c, k)
-        copy = remote(part.at[col], rs_buf.at[k - 1], rs_s.at[k - 1], rs_r.at[k - 1], s, col)
-        copy.start()
-        rs_copies.append(copy)
+        hphi[9 * (p // 3) + 3 + p % 3] = (base[p] - 0.5 * (low + high)).astype(BF16)
+    h_mid = products(table, 6, 3, hphi, phi, None)
+
     total = part[c]
     for k in range(1, n):
         rs_copies[k - 1].wait_recv()
@@ -288,13 +285,13 @@
         copy = remote(piece, ag.at[c], ag_s.at[k - 1], ag_r.at[k - 1], s, up(c, k))
         copy.start()
         ag_copies.append(copy)
+    h_low = products(table, 0, 6, hphi, phi, bl)
     for copy in kn_copies:
         copy.wait_recv()
     panel = split(jnp.concatenate([unpack(k0n[0]), k0[...], unpack(k0n[1])], axis=0))
     for copy in ag_copies:
         copy.wait_recv()
-    for a in range(ATOMS):
-        mrow[4 * a : 4 * a + 4, :] = ag[a, 0:4, :]
+    from_pieces(ag, mrow)
     m_own = mrow[...]
     bblk[...] = pack(dot3(split(m_own), panel))
     b_copies = []
@@ -303,6 +300,19 @@
         copy.start()
         b_copies.append(copy)
     ball[s] = bblk[...]
+    h_up = products(table, 9, 6, hphi, phi, bu)
+    to_pieces(
+        part_h,
+        jnp.concatenate(
+            [h_low[:, ROWS:], h_low[:, :ROWS] + h_mid + h_up[:, :ROWS], h_up[:, ROWS:]], axis=1
+        ),
+    )
+    rh_copies = []
+    for k in range(1, n):
+        col = up(c, k)
+        copy = remote(part_h.at[col], rs_buf_h.at[k - 1], rh_s.at[k - 1], rh_r.at[k - 1], s, col)
+        copy.start()
+        rh_copies.append(copy)
     inside = jnp.where(active, 1.0, 0.0).astype(F32)
 
     def block(matrix):
@@ -310,8 +320,6 @@
         return jnp.where(e == 0, left, jnp.where(e == 1, mid, right)) * inside
 
     out[0] = block(m_own)
-    for a in range(ATOMS):
-        out[1, 4 * a : 4 * a + 4, :] = block(ag[a, 4:8, :])
 
     for copy in kr_copies:
         copy.wait_recv()
@@ -344,10 +352,28 @@
             copy.start()
 
     out[2] = jnp.zeros((ROWS, ROWS), F32)
+    out[1] = jnp.zeros((ROWS, ROWS), F32)
+    total_h = part_h[c]
+    for k in range(1, n):
+        rh_copies[k - 1].wait_recv()
+        total_h = total_h + rs_buf_h[k - 1]
+    piece_h[...] = total_h
+    h_sends = []
+    for i in range(3):
+        target = up(s, i - 1)
+        wanted = target != c
+        copy = remote(piece_h, ag_h.at[c], ah_s.at[i], ah_r.at[c], s, target)
+        h_sends.append((wanted, copy))
+
+        @pl.when(wanted)
+        def _():
+            copy.start()
+
 
     @pl.when(active)
     def _():
         y1all[c] = y1[...]
+        ag_h[c] = piece_h[...]
         for k in range(1, n):
             other = up(c, k)
             remote(y1, y1all.at[other], y_s.at[0], y_r.at[other], s, other).wait_recv()
@@ -372,6 +398,11 @@
             def _():
                 remote(k1, k1all.at[i], k_s.at[i], k_r.at[i], t, v).wait_recv()
 
+        for k in range(1, n):
+            other = up(c, k)
+            remote(piece_h, ag_h.at[other], ah_s.at[0], ah_r.at[other], s, other).wait_recv()
+        from_pieces(ag_h, hrow)
+        out[1] = block(hrow[...])
         kb = {}
         mb = {}
         for r in range(5):
@@ -406,9 +437,9 @@
             def _():
                 remote(k1, k1all.at[(2 - d) * 3 + e], k_s.at[i], k_r.at[i], t, v).wait_send()
 
-    for copy in halo + band_copies + rs_copies + kn_copies + kr_copies + ag_copies + b_copies:
+    for copy in halo + band_copies + rs_copies + rh_copies + kn_copies + kr_copies + ag_copies + b_copies:
         copy.wait_send()
-    for wanted, copy in m_sends + y_sends:
+    for wanted, copy in m_sends + y_sends + h_sends:
 
         @pl.when(wanted)
         def _():
@@ -432,18 +463,24 @@
         ],
         out_specs=vmem,
         scratch_shapes=[
-            blocks(90, 2 * ROWS),
+            blocks(90),
+            blocks(90),
             blocks(63),
             blocks(63),
             blocks(27),
             blocks(27),
             blocks(27, kind=F32),
             blocks(27, ATOMS),
-            pltpu.VMEM((n, 8, 3 * ROWS), F32),
+            pltpu.VMEM((n, 8, 2 * ROWS), F32),
             half(),
-            pltpu.VMEM((n - 1, 8, 3 * ROWS), F32),
-            pltpu.VMEM((8, 3 * ROWS), F32),
-            pltpu.VMEM((n, 8, 3 * ROWS), F32),
+            pltpu.VMEM((n - 1, 8, 2 * ROWS), F32),
+            pltpu.VMEM((8, 2 * ROWS), F32),
+            pltpu.VMEM((n, 8, 2 * ROWS), F32),
+            pltpu.VMEM((n, 8, 2 * ROWS), F32),
+            pltpu.VMEM((n - 1, 8, 2 * ROWS), F32),
+            pltpu.VMEM((8, 2 * ROWS), F32),
+            pltpu.VMEM((n, 8, 2 * ROWS), F32),
+            pltpu.VMEM((ROWS, 3 * ROWS), F32),
             half(n),
             half(2),
             half(),
@@ -456,7 +493,8 @@
             pltpu.VMEM((5, ROWS, 3 * ROWS), F32),
             dma, dma((12,)), dma((12,)), dma((2,)), dma((2,)),
             pltpu.SemaphoreType.REGULAR((6,)),
-            dma((n,)), dma((n,)), dma((n,)), dma((n,)), dma((n,)), dma((n,)),
+            dma((n,)), dma((n,)), dma((n,)), dma((n,)), dma((n,)), dma((n,)), dma((3,)), dma((n,)),
+            dma((n,)), dma((n,)),
             dma((2,)), dma((2,)), dma((n,)), dma((n,)), dma((3,)), dma((n,)),
             dma((15,)), dma((15,)), dma((4,)), dma((4,)),
         ],

time: 74.5 us -> 68.7 us (0.922)
  Pallas kernels: 69.1 us -> 63.3 us
    pallas_call x1, Pallas kernels: 69.1 us -> 63.3 us  [slab_program(): pl.pallas_call(functools.partial(slab_kernel, n), out_shape=jax.ShapeDtyp...]
where the time goes in v4:
time: 68.7 us; the launch traced here: 68.5 us
  Pallas kernels  63.3 us (92%)
  local copies, waits for them, and re-layouts  3.9 us (6%)
  between operations  0.76 us (1%)
    pallas_call x1, Pallas kernels, slab_program(): pl.pallas_call(functools.partial(slab_kernel, n), out_shape=jax.ShapeDtyp...  63.3 us
    transpose x1, local copies, waits for them, and re-layouts, local(): x = supports.transpose(2, 3, 0, 1, 4).reshape(27, ROWS, 256)  1.62 us

profile of v4, /device:TPU:1, one launch (start us, length us, event | category | flops | bytes accessed | tf_op | source)
XLA Modules:
  0.0 68.5 jit_solution(3525353518705026766)
XLA Ops:
  0.6 0.0 copy-start.2
  0.7 0.1 pad_dynamic-slice_fusion.1
  0.8 0.6 copy-done.2
  1.3 0.1 fusion.9
  1.4 0.1 broadcast_subtract_fusion
  1.6 0.1 and_reduce_fusion
  1.6 0.1 slice_select_fusion.1
  1.7 0.1 pad_add_fusion
  1.8 0.1 reshape.87.table
  1.9 1.6 %copy.11 = bf16[27,1,16,4,256]{4,3,2,0,1:T(4,128)(2,1)S(1)} copy(bf16[27,1,16,4,256]{4,3,1,0,2:T(4,128)(2,1)} %bitcast.21) | data formatting | bytes 1769472 | tf_op jit(solution)/shard_map/transpose | solution.py:523
  3.5 0.0 copy-start
  3.5 0.2 reshape.88.x_ref
  3.7 0.0 copy-start.1
  3.8 0.1 constant_dynamic-slice_fusion.1
  3.8 0.1 fusion
  3.9 0.5 copy-done
  4.5 0.1 copy-done.1
  4.5 63.3 %shard_map.67 = f32[3,64,64]{2,1,0:T(8,128)S(1)} custom-call(s32[15,64]{1,0:T(8,128)S(1)} %reshape.87.table, bf16[27,64,256]{2,1,0:T(8,128)(2,1)S(1)} %reshape.88.x_ref, bf16[27,16,256]{2,1,0:T(8,128)(2,1)S(1)} %bitcast.20, f32[64,64]{1,0:T(8,128)S(1)} %copy-done.1, f32[16,16]{1,0:T(8,128)S(1)} %convert_element_type.3.near), custom_call_target="tpu_custom_call" | custom-call | tf_op jit(solution)/shard_map/pallas_call | solution.py:454
  67.9 0.6 slice_bitcast_fusion
  (9 shorter events, 0.1 us)
Async XLA Ops:
  0.6 0.7 %copy-start.2 = (s32[256,3]{0,1:T(4,128)S(1)}, s32[256,3]{0,1:T(4,128)}, u32[]{:S(2)}) copy-start(s32[256,3]{0,1:T(4,128)} %param.6) | copy-start | bytes 9220
  3.5 0.9 %copy-start = (bf16[16,27,1,256]{3,0,2,1:T(8,128)(2,1)S(1)}, bf16[16,27,1,256]{3,0,2,1:T(8,128)(2,1)}, u32[]{:S(2)}) copy-start(bf16[16,27,1,256]{3,0,2,1:T(8,128)(2,1)} %param.5) | copy-start | bytes 663556
  3.7 0.8 %copy-start.1 = (f32[64,64]{1,0:T(8,128)S(1)}, f32[64,64]{1,0:T(8,128)}, u32[]{:S(2)}) copy-start(f32[64,64]{1,0:T(8,128)} %k0.1) | copy-start | bytes 49156

commit v5 on v4

--- a/solution.py
+++ b/solution.py
@@ -177,28 +177,36 @@
         pl.semaphore_wait(known.at[3 + step], 2)
 
     tell(0)
-    halo = [
-        remote(x_ref, lo, halo_s.at[0], halo_r.at[0], s, up(c, 1)),
-        remote(x_ref, hi, halo_s.at[1], halo_r.at[1], s, up(c, -1)),
-    ]
-    for copy in halo:
-        copy.start()
-    band_copies = []
-    for k in range(6):
-        source, target = x_ref.at[9 + 3 * k : 12 + 3 * k], bl.at[9 * k + 3 : 9 * k + 6]
-        band_copies.append(remote(source, target, band_s.at[k], band_r.at[k], up(s, 1), c))
-        source, target = x_ref.at[3 * k : 3 * k + 3], bu.at[9 * k + 3 : 9 * k + 6]
-        band_copies.append(remote(source, target, band_s.at[6 + k], band_r.at[6 + k], up(s, -1), c))
-    for copy in band_copies:
-        copy.start()
     kn_copies = []
     for i, d in enumerate((1, -1)):
         copy = remote(k0p, k0n.at[i], kn_s.at[i], kn_r.at[i], up(s, d), c)
         copy.start()
         kn_copies.append(copy)
-
+    halo = []
+    band_copies = []
+
+    def bulk(part_of):
+        at = 9 * part_of
+        copies = [
+            remote(x_ref.at[at : at + 9], lo.at[at : at + 9], halo_s.at[part_of], halo_r.at[part_of], s, up(c, 1)),
+            remote(
+                x_ref.at[at : at + 9], hi.at[at : at + 9], halo_s.at[3 + part_of], halo_r.at[3 + part_of], s, up(c, -1)
+            ),
+        ]
+        halo.extend(copies)
+        for k in (2 * part_of, 2 * part_of + 1):
+            source, target = x_ref.at[9 + 3 * k : 12 + 3 * k], bl.at[9 * k + 3 : 9 * k + 6]
+            down = remote(source, target, band_s.at[k], band_r.at[k], up(s, 1), c)
+            source, target = x_ref.at[3 * k : 3 * k + 3], bu.at[9 * k + 3 : 9 * k + 6]
+            copies.extend([down, remote(source, target, band_s.at[6 + k], band_r.at[6 + k], up(s, -1), c)])
+        band_copies.extend(copies[2:])
+        for copy in copies:
+            copy.start()
+
+    bulk(0)
     learn(0)
     tell(1)
+    bulk(1)
     own, z_low, z_high, y_low, y_high = shift_matrices()
     for bx in range(3):
         first = 9 * bx
@@ -210,20 +218,13 @@
             base[first + f : first + f + 2] += mm(rows(f + 1, 2), z_high).reshape(2, ROWS, 256)
         base[first + 3 : first + 9] += mm(rows(0, 6), y_low).reshape(6, ROWS, 256)
         base[first : first + 6] += mm(rows(3, 6), y_high).reshape(6, ROWS, 256)
-        if bx == 0:
-            learn(1)
-            tell(2)
+    learn(1)
+    tell(2)
+    bulk(2)
     spread = (
         lax.broadcasted_iota(jnp.int32, (ROWS, ATOMS), 0) // FUNCS
         == lax.broadcasted_iota(jnp.int32, (ROWS, ATOMS), 1)
     ).astype(F32).astype(BF16)
-    learn(2)
-    kr_copies = []
-    for k in range(1, n):
-        copy = remote(k0p, k0row.at[c], kr_s.at[k - 1], kr_r.at[k - 1], s, up(c, k))
-        copy.start()
-        kr_copies.append(copy)
-    k0row[c] = k0p[...]
     load.wait()
     for p in range(27):
         base[p] = -0.5 * base[p] + mm(spread, v_ref[p]) * x_ref[p].astype(F32)
@@ -245,6 +246,13 @@
         (((1,), (1,)), ((), ())),
         preferred_element_type=F32,
     )
+    learn(2)
+    kr_copies = []
+    for k in range(1, n):
+        copy = remote(k0p, k0row.at[c], kr_s.at[k - 1], kr_r.at[k - 1], s, up(c, k))
+        copy.start()
+        kr_copies.append(copy)
+    k0row[c] = k0p[...]
     s_own = products(table, 0, 15, phi, phi, None)
     for copy in band_copies:
         copy.wait_recv()
@@ -300,19 +308,6 @@
         copy.start()
         b_copies.append(copy)
     ball[s] = bblk[...]
-    h_up = products(table, 9, 6, hphi, phi, bu)
-    to_pieces(
-        part_h,
-        jnp.concatenate(
-            [h_low[:, ROWS:], h_low[:, :ROWS] + h_mid + h_up[:, :ROWS], h_up[:, ROWS:]], axis=1
-        ),
-    )
-    rh_copies = []
-    for k in range(1, n):
-        col = up(c, k)
-        copy = remote(part_h.at[col], rs_buf_h.at[k - 1], rh_s.at[k - 1], rh_r.at[k - 1], s, col)
-        copy.start()
-        rh_copies.append(copy)
     inside = jnp.where(active, 1.0, 0.0).astype(F32)
 
     def block(matrix):
@@ -353,6 +348,38 @@
 
     out[2] = jnp.zeros((ROWS, ROWS), F32)
     out[1] = jnp.zeros((ROWS, ROWS), F32)
+    h_up = products(table, 9, 6, hphi, phi, bu)
+    to_pieces(
+        part_h,
+        jnp.concatenate(
+            [h_low[:, ROWS:], h_low[:, :ROWS] + h_mid + h_up[:, :ROWS], h_up[:, ROWS:]], axis=1
+        ),
+    )
+    rh_copies = []
+    for k in range(1, n):
+        col = up(c, k)
+        copy = remote(part_h.at[col], rs_buf_h.at[k - 1], rh_s.at[k - 1], rh_r.at[k - 1], s, col)
+        copy.start()
+        rh_copies.append(copy)
+
+    @pl.when(active)
+    def _():
+        y1all[c] = y1[...]
+        for k in range(1, n):
+            other = up(c, k)
+            remote(y1, y1all.at[other], y_s.at[0], y_r.at[other], s, other).wait_recv()
+        ycat = split(side_by_side(y1all, n))
+        first = mask * (3.0 * y_own - 2.0 * dot3(ycat, bcol))
+        k1[...] = pack(first)
+        for i, (d, f) in enumerate(pairs):
+            t, v = up(s, d), up(s, d + f - 1)
+
+            @pl.when(jnp.logical_not((d == 0) & (v == c)))
+            def _():
+                remote(k1, k1all.at[(2 - d) * 3 + e], k_s.at[i], k_r.at[(2 - d) * 3 + e], t, v).start()
+
+        k1all[6 + e] = k1[...]
+
     total_h = part_h[c]
     for k in range(1, n):
         rh_copies[k - 1].wait_recv()
@@ -369,25 +396,9 @@
         def _():
             copy.start()
 
-
     @pl.when(active)
     def _():
-        y1all[c] = y1[...]
         ag_h[c] = piece_h[...]
-        for k in range(1, n):
-            other = up(c, k)
-            remote(y1, y1all.at[other], y_s.at[0], y_r.at[other], s, other).wait_recv()
-        ycat = split(side_by_side(y1all, n))
-        first = mask * (3.0 * y_own - 2.0 * dot3(ycat, bcol))
-        k1[...] = pack(first)
-        for i, (d, f) in enumerate(pairs):
-            t, v = up(s, d), up(s, d + f - 1)
-
-            @pl.when(jnp.logical_not((d == 0) & (v == c)))
-            def _():
-                remote(k1, k1all.at[(2 - d) * 3 + e], k_s.at[i], k_r.at[(2 - d) * 3 + e], t, v).start()
-
-        k1all[6 + e] = k1[...]
         mall[2] = m_own
         for i, d in enumerate((-2, -1, 1, 2)):
             remote(mrow, mall.at[2 - d], m_s.at[i], m_r.at[i], up(s, d), c).wait_recv()
@@ -398,11 +409,6 @@
             def _():
                 remote(k1, k1all.at[i], k_s.at[i], k_r.at[i], t, v).wait_recv()
 
-        for k in range(1, n):
-            other = up(c, k)
-            remote(piece_h, ag_h.at[other], ah_s.at[0], ah_r.at[other], s, other).wait_recv()
-        from_pieces(ag_h, hrow)
-        out[1] = block(hrow[...])
         kb = {}
         mb = {}
         for r in range(5):
@@ -430,6 +436,11 @@
             e == 0, y2[:, 2 * ROWS : 3 * ROWS], jnp.where(e == 1, y2[:, 3 * ROWS : 4 * ROWS], y2[:, 4 * ROWS : 5 * ROWS])
         )
         out[2] = mask * (3.0 * y2s - 2.0 * dot3(split(w2), split(kcol)))
+        for k in range(1, n):
+            other = up(c, k)
+            remote(piece_h, ag_h.at[other], ah_s.at[0], ah_r.at[other], s, other).wait_recv()
+        from_pieces(ag_h, hrow)
+        out[1] = block(hrow[...])
         for i, (d, f) in enumerate(pairs):
             t, v = up(s, d), up(s, d + f - 1)
 
@@ -491,7 +502,7 @@
             half(15),
             pltpu.VMEM((ROWS, 3 * ROWS), F32),
             pltpu.VMEM((5, ROWS, 3 * ROWS), F32),
-            dma, dma((12,)), dma((12,)), dma((2,)), dma((2,)),
+            dma, dma((12,)), dma((12,)), dma((6,)), dma((6,)),
             pltpu.SemaphoreType.REGULAR((6,)),
             dma((n,)), dma((n,)), dma((n,)), dma((n,)), dma((n,)), dma((n,)), dma((3,)), dma((n,)),
             dma((n,)), dma((n,)),

time: 68.7 us -> 68.6 us (level)
  no operation moved by 1% of the time
where the time goes in v5:
time: 68.6 us; the launch traced here: 68.4 us
  Pallas kernels  63.2 us (92%)
  local copies, waits for them, and re-layouts  3.9 us (6%)
  between operations  0.76 us (1%)
    pallas_call x1, Pallas kernels, slab_program(): pl.pallas_call(functools.partial(slab_kernel, n), out_shape=jax.ShapeDtyp...  63.2 us
    transpose x1, local copies, waits for them, and re-layouts, local(): x = supports.transpose(2, 3, 0, 1, 4).reshape(27, ROWS, 256)  1.62 us

profile of v5, /device:TPU:1, one launch (start us, length us, event | category | flops | bytes accessed | tf_op | source)
XLA Modules:
  0.0 68.4 jit_solution(18225793563094175723)
XLA Ops:
  0.6 0.0 copy-start.2
  0.7 0.1 pad_dynamic-slice_fusion.1
  0.8 0.6 copy-done.2
  1.3 0.1 fusion.9
  1.4 0.1 broadcast_subtract_fusion
  1.6 0.1 and_reduce_fusion
  1.6 0.1 slice_select_fusion.1
  1.7 0.1 pad_add_fusion
  1.8 0.1 reshape.87.table
  1.9 1.6 %copy.11 = bf16[27,1,16,4,256]{4,3,2,0,1:T(4,128)(2,1)S(1)} copy(bf16[27,1,16,4,256]{4,3,1,0,2:T(4,128)(2,1)} %bitcast.21) | data formatting | bytes 1769472 | tf_op jit(solution)/shard_map/transpose | solution.py:534
  3.5 0.0 copy-start
  3.5 0.2 reshape.88.x_ref
  3.7 0.0 copy-start.1
  3.8 0.1 constant_dynamic-slice_fusion.1
  3.8 0.1 fusion
  3.9 0.5 copy-done
  4.5 0.1 copy-done.1
  4.5 63.2 %shard_map.67 = f32[3,64,64]{2,1,0:T(8,128)S(1)} custom-call(s32[15,64]{1,0:T(8,128)S(1)} %reshape.87.table, bf16[27,64,256]{2,1,0:T(8,128)(2,1)S(1)} %reshape.88.x_ref, bf16[27,16,256]{2,1,0:T(8,128)(2,1)S(1)} %bitcast.20, f32[64,64]{1,0:T(8,128)S(1)} %copy-done.1, f32[16,16]{1,0:T(8,128)S(1)} %convert_element_type.3.near), custom_call_target="tpu_custom_call" | custom-call | tf_op jit(solution)/shard_map/pallas_call | solution.py:465
  67.8 0.6 slice_bitcast_fusion
  (9 shorter events, 0.1 us)
Async XLA Ops:
  0.6 0.7 %copy-start.2 = (s32[256,3]{0,1:T(4,128)S(1)}, s32[256,3]{0,1:T(4,128)}, u32[]{:S(2)}) copy-start(s32[256,3]{0,1:T(4,128)} %param.6) | copy-start | bytes 9220
  3.5 0.9 %copy-start = (bf16[16,27,1,256]{3,0,2,1:T(8,128)(2,1)S(1)}, bf16[16,27,1,256]{3,0,2,1:T(8,128)(2,1)}, u32[]{:S(2)}) copy-start(bf16[16,27,1,256]{3,0,2,1:T(8,128)(2,1)} %param.5) | copy-start | bytes 663556
  3.7 0.8 %copy-start.1 = (f32[64,64]{1,0:T(8,128)S(1)}, f32[64,64]{1,0:T(8,128)}, u32[]{:S(2)}) copy-start(f32[64,64]{1,0:T(8,128)} %k0.1) | copy-start | bytes 49156
